TPU v7x, 32 devices: a whole 2x2x4 slice. The times are simulated.
32 devices in a mesh: tilt: 8 (over z, y), tile: 4 (over x, core).
Axes of the slice: x: 2, y: 2, z: 4, core: 2. Of those that a mesh axis runs over, the one named last changes fastest.
Arguments:
- images: float32 [16, 1024, 4096], P('tilt', 'tile'), may hold values from -6 to 6
- taps: float32 [9], replicated, may hold values from -3 to 3
- shifts: int32 [16, 2], P('tilt'), may hold values from -4 to 4
- patch_rows: int32 [16, 16], P('tilt'), may hold values from 0 to 1023
- patch_cols: int32 [16, 16], P('tilt'), may hold values from 0 to 4095
- rows_interp: float32 [64, 1024], P(None, 'tile'), may hold values from -0.1875 to 0.1875
- cols_interp: float32 [64, 4096], replicated, may hold values from -0.09375 to 0.09375
Outputs:
- warps: float32 [16, 64, 64], P('tilt', 'tile')
Inputs may be any that keep to these rules, and one draw needn't show every extreme that they name: Row and column shifts lie within plus or minus 4. `patch_rows`: patch centres lie inside the image. `patch_cols`: patch centres lie inside the image.
All inputs are finite; a program needn't handle non-finite values.
Results may differ from a plain program's by a relative error of at most 0.0003.
Values sent between devices are 32-bit elements; how exact they have to be, the bound alone decides.
A program may use at most 128 MiB of HBM per device.

v0:
```python
import jax
import jax.numpy as jnp
from jax import lax
from jax.sharding import PartitionSpec as P

NODES = 64
RAD = 4
SMAX = 4
PATCH_HALF = 256
PASSES = 2


epsilon = 1e-06


def with_halo(block, sides, width):
    for axis, dim in sides:
        count = lax.axis_size(axis)
        forward = [(i, i + 1) for i in range(count - 1)]
        backward = [(target, source) for source, target in forward]
        low = lax.ppermute(
            lax.slice_in_dim(block, block.shape[dim] - width, None, axis=dim), axis, forward
        )
        high = lax.ppermute(lax.slice_in_dim(block, 0, width, axis=dim), axis, backward)
        block = jnp.concatenate([low, block, high], axis=dim)
    return block


def shifted(value, axis, steps):
    count = lax.axis_size(axis)
    initial, last = (max(0, -steps), min(count, count - steps))
    return lax.ppermute(value, axis, [(source, source + steps) for source in range(initial, last)])


def carried_in(value, axis, combine, identity):
    devices, place = (lax.axis_size(axis), lax.axis_index(axis))
    everything = lax.all_gather(value, axis)
    start = jnp.broadcast_to(jnp.asarray(identity, value.dtype), value.shape)

    def step(k, before):
        reached = k < place
        new = combine(before, everything[k])
        return jnp.where(reached, new, before)

    return lax.fori_loop(0, devices, step, start)


def filter_columns(stack, taps):
    columns = stack.shape[-1]
    padding = [(0, 0)] * (stack.ndim - 1) + [(RAD, RAD)]
    padded = jnp.pad(stack, padding)
    total = taps[0] * padded[..., 0:columns]
    for offset in range(1, 2 * RAD + 1):
        total = total + taps[offset] * padded[..., offset : offset + columns]
    return total


def filter_rows_valid(stack, taps):
    count = stack.shape[-2] - 2 * RAD
    total = taps[0] * stack[..., 0:count, :]
    for offset in range(1, 2 * RAD + 1):
        total = total + taps[offset] * stack[..., offset : offset + count, :]
    return total


def shards(images, taps, shifts, patch_rows, patch_cols, rows_interp, cols_interp):
    highest = lax.Precision.HIGHEST
    tilt_count, band_rows, columns = images.shape
    tile_count = lax.axis_size("tile")
    total_rows = band_rows * tile_count
    band_start = lax.axis_index("tile") * band_rows
    margin = RAD + SMAX
    banded = with_halo(images, (("tile", 1),), margin)
    ext_global = band_start - SMAX + jnp.arange(band_rows + 2 * SMAX, dtype=jnp.int32)
    inside = ((ext_global >= 0) & (ext_global < total_rows)).astype(jnp.float32)[:, None]
    filtered = filter_rows_valid(filter_columns(banded, taps), taps) * inside
    raw_next = shifted(banded[0], "tilt", -1)
    following = filter_rows_valid(filter_columns(raw_next, taps), taps) * inside
    partners = jnp.concatenate([filtered[1:], following[None]], axis=0)

    def move_one(extended, shift_pair):
        padded = jnp.pad(extended, ((0, 0), (SMAX, SMAX)))
        return lax.dynamic_slice(
            padded, (SMAX + shift_pair[0], SMAX + shift_pair[1]), (band_rows, columns)
        )

    moved = jax.vmap(move_one)(partners, shifts)
    current = filtered[:, SMAX : SMAX + band_rows, :]
    differ = moved - current
    side = jnp.pad(current, ((0, 0), (0, 0), (1, 1)))
    slope = 0.5 * (side[..., 2:] - side[..., :-2])
    row_global = band_start + jnp.arange(band_rows, dtype=jnp.int32)
    col_global = jnp.arange(columns, dtype=jnp.int32)
    row_boxes = (jnp.abs(row_global[None, None, :] - patch_rows[:, :, None]) <= PATCH_HALF).astype(
        jnp.bfloat16
    )
    col_boxes = (jnp.abs(col_global[None, None, :] - patch_cols[:, :, None]) <= PATCH_HALF).astype(
        jnp.bfloat16
    )
    counts = jnp.einsum("tpr,tpc->trc", row_boxes, col_boxes, preferred_element_type=jnp.float32)
    tilt_global = lax.axis_index("tilt") * tilt_count + jnp.arange(tilt_count, dtype=jnp.int32)
    valid = (tilt_global < tilt_count * lax.axis_size("tilt") - 1).astype(jnp.float32)
    weights = counts * valid[:, None, None]
    grids = jnp.zeros((tilt_count, NODES, NODES), jnp.float32)
    field = jnp.zeros((tilt_count, band_rows, columns), jnp.float32)
    for step in range(PASSES):
        resid = differ + slope * field
        weighted = weights * slope * resid
        left_part = jnp.einsum("nr,trc->tnc", rows_interp, weighted, precision=highest)
        partial_grad = jnp.einsum("tnc,mc->tnm", left_part, cols_interp, precision=highest)
        grad = lax.psum(partial_grad, "tile")
        grad_sq = jnp.sum(grad * grad, axis=(1, 2))
        row_part = jnp.einsum("nr,tnm->trm", rows_interp, grad, precision=highest)
        image_dir = jnp.einsum("trm,mc->trc", row_part, cols_interp, precision=highest)
        along = slope * image_dir
        curv = lax.psum(jnp.sum(weights * along * along, axis=(1, 2)), "tile")
        alpha = grad_sq / (curv + epsilon)
        grids = grids - alpha[:, None, None] * grad
        field = field - alpha[:, None, None] * image_dir
    share = NODES // tile_count
    mine = lax.dynamic_slice_in_dim(grids, lax.axis_index("tile") * share, share, 1)
    running = jnp.cumsum(mine, axis=0)
    block_total = running[-1]

    def combine(earlier, later):
        return earlier + later

    before = carried_in(block_total, "tilt", combine, jnp.zeros_like(block_total))
    return before[None] + (running - mine)


def solution(mesh):
    return jax.shard_map(
        shards,
        mesh=mesh,
        in_specs=(
            P("tilt", "tile", None),
            P(),
            P("tilt", None),
            P("tilt", None),
            P("tilt", None),
            P(None, "tile"),
            P(),
        ),
        out_specs=P("tilt", "tile", None),
        check_vma=False,
    )
```

profile of v0, /device:TPU:0, one launch (start us, length us, event | category | flops | bytes accessed | tf_op | source)
XLA Modules:
  0.0 313.1 jit_solution(16856051781107647198)
XLA Ops:
  0.0 0.0 copy-start
  0.0 1.2 fusion.88
  1.2 2.4 collective-permute-start
  3.6 1.3 collective-permute-start.1
  4.9 0.8 compare_select_fusion.1
  5.7 0.1 pad_add_fusion
  5.8 5.3 %fusion.64 = f32[2,256,4096]{2,1,0:T(8,128)} fusion(s32[2,16]{1,0:T(2,128)} %param.13, s32[2,16]{1,0:T(2,128)} %param.12, s32[256]{0:T(256)S(1)} %iota_add_fusion.1), kind=kOutput, calls=%fused_computation.100 | convolution fusion | flops 67526656 | bytes 8389888 | tf_op jit(solution)/shard_map/tpr,tpc->trc/dot_general | solution.py:100
  11.1 0.0 copy-done.4
  11.1 0.7 fusion.89
  11.8 0.0 collective-permute-done
  11.8 3.9 %constant_dynamic-update-slice_fusion.1 = f32[2,272,4096]{2,1,0:T(8,128)S(1)} fusion(f32[2,272,4096]{2,1,0:T(8,128)S(1)} %constant_dynamic-update-slice_fusion.2, f32[2,256,4096]{2,1,0:T(8,128)} %param.9), kind=kLoop, calls=%fused_computation.119 | loop fusion | bytes 16777216
  15.8 0.0 collective-permute-done.1
  15.8 2.6 slice_bitcast_fusion
  18.4 1.8 collective-permute-start.2
  20.2 0.4 copy-done.2
  20.7 47.4 %multiply_add_fusion = f32[2,272,4096]{2,1,0:T(8,128)S(1)} fusion(f32[2,272,4096]{2,1,0:T(8,128)} %copy-done.2, f32[]{:T(128)} %bitcast.8, f32[]{:T(128)} %bitcast.7, f32[]{:T(128)} %bitcast.6, f32[]{:T(128)} %bitcast.5, f32[]{:T(128)} %bitcast.4, f32[]{:T(128)} %bitcast.3, f32[]{:T(128)} %bitcast.2, f32[]{:T(128)} %bitcast.1, f32[]{:T(128)} %bitcast), kind=kLoop, calls=%fused_computation.9 | loop fusion | flops 37879808 | bytes 17825828 | tf_op jit(solution)/shard_map/add | solution.py:54
  68.0 16.0 %fusion.7 = f32[2,264,4096]{2,1,0:T(8,128)} fusion(f32[2,272,4096]{2,1,0:T(8,128)S(1)} %multiply_add_fusion, f32[264]{0:T(512)S(1)} %fusion.79, f32[]{:T(128)} %bitcast.8, f32[]{:T(128)} %bitcast.7, f32[]{:T(128)} %bitcast.6, f32[]{:T(128)} %bitcast.5, f32[]{:T(128)} %bitcast.4, f32[]{:T(128)} %bitcast.3, f32[]{:T(128)} %bitcast.2, f32[]{:T(128)} %bitcast.1, ...), kind=kLoop, calls=%fused_computation.20 | loop fusion | flops 38928384 | bytes 86508608 | tf_op jit(solution)/shard_map/mul | solution.py:76
  84.0 3.5 %copy-done.1 = f32[2,264,4096]{2,1,0:T(8,128)S(1)} copy-done((f32[2,264,4096]{2,1,0:T(8,128)S(1)}, f32[2,264,4096]{2,1,0:T(8,128)}, u32[]{:S(2)}) %copy-start.1) | copy-done | bytes 8650776
  87.5 1.5 slice.264
  89.0 6.5 %slice_subtract_fusion = f32[2,256,4096]{2,1,0:T(8,128)} fusion(f32[2,256,4096]{2,1,0:T(8,128)S(1)} %slice.264), kind=kLoop, calls=%fused_computation.48 | loop fusion | flops 2097152 | bytes 16777216 | tf_op jit(solution)/shard_map/sub | solution.py:91
  95.5 22.6 %collective-permute-done.2 = f32[272,4096]{1,0:T(8,128)} collective-permute-done((f32[272,4096]{1,0:T(8,128)}, f32[272,4096]{1,0:T(8,128)}, u32[]{:S(2)}, u32[]{:S(2)}) %collective-permute-start.2) | collective-permute-done | bytes 4456480 | tf_op jit(solution)/shard_map/ppermute | solution.py:32
  118.1 28.6 %multiply_add_fusion.1 = f32[272,4096]{1,0:T(8,128)S(1)} fusion(f32[272,4096]{1,0:T(8,128)} %collective-permute-done.2, f32[]{:T(128)} %bitcast.8, f32[]{:T(128)} %bitcast.7, f32[]{:T(128)} %bitcast.6, f32[]{:T(128)} %bitcast.5, f32[]{:T(128)} %bitcast.4, f32[]{:T(128)} %bitcast.3, f32[]{:T(128)} %bitcast.2, f32[]{:T(128)} %bitcast.1, f32[]{:T(128)} %bitcast), kind=kLoop, calls=%fused_computation.55 | loop fusion | flops 18939904 | bytes 8912932 | tf_op jit(solution)/shard_map/add | solution.py:54
  146.7 0.0 slice-start
  146.7 11.7 %fusion.42 = f32[1,264,4096]{2,1,0:T(8,128)} fusion(f32[272,4096]{1,0:T(8,128)S(1)} %multiply_add_fusion.1, f32[264]{0:T(512)S(1)} %fusion.79, f32[]{:T(128)} %bitcast.8, f32[]{:T(128)} %bitcast.7, f32[]{:T(128)} %bitcast.6, f32[]{:T(128)} %bitcast.5, f32[]{:T(128)} %bitcast.4, f32[]{:T(128)} %bitcast.3, f32[]{:T(128)} %bitcast.2, f32[]{:T(128)} %bitcast.1, ...), kind=kLoop, calls=%fused_computation.67 | loop fusion | flops 19464192 | bytes 43254852 | tf_op jit(solution)/shard_map/broadcast_in_dim | solution.py:79
  158.4 6.8 %select_maximum_fusion = f32[2,264,4104]{2,1,0:T(8,128)} fusion(f32[1,264,4096]{2,1,0:T(8,128)} %fusion.42, f32[1,264,4096]{2,1,0:T(8,128)S(1)} %slice-done), kind=kLoop, calls=%fused_computation.7 | loop fusion | flops 13001472 | bytes 17318400 | tf_op jit(solution)/shard_map/concatenate | solution.py:79
  165.1 15.7 %while.17 = (s32[]{:T(128)}, f32[2,264,4104]{2,1,0:T(8,128)}, s32[2,3]{1,0:T(2,128)S(1)}, f32[2,256,4096]{2,1,0:T(8,128)}) while((s32[]{:T(128)}, f32[2,264,4104]{2,1,0:T(8,128)}, s32[2,3]{1,0:T(2,128)S(1)}, f32[2,256,4096]{2,1,0:T(8,128)}) %tuple.65), condition=%wide.while_cond.clone, body=%wide.while_body.sunk.clone | while | flops 2 | bytes 8390761 | solution.py:83
  165.2 0.6 fusion.98
  165.8 7.3 %dynamic-slice_dynamic-update-slice_fusion.3 = f32[2,256,4096]{2,1,0:T(8,128)} fusion(f32[2,256,4096]{2,1,0:T(8,128)} %get-tuple-element.229, s32[]{:T(128)} %get-tuple-element.226, f32[2,264,4104]{2,1,0:T(8,128)} %get-tuple-element.231, s32[]{:T(128)} %bitcast.60, s32[]{:T(128)} %bitcast.61, s32[]{:T(128)} %bitcast.62), kind=kLoop, calls=%fused_computation.clone.1.clone | loop fusion | bytes 8390656 | tf_op jit(solution)/shard_map/vmap()/gather
  173.0 0.6 fusion.98
  173.7 7.2 %dynamic-slice_dynamic-update-slice_fusion.3 = f32[2,256,4096]{2,1,0:T(8,128)} fusion(f32[2,256,4096]{2,1,0:T(8,128)} %get-tuple-element.229, s32[]{:T(128)} %get-tuple-element.226, f32[2,264,4104]{2,1,0:T(8,128)} %get-tuple-element.231, s32[]{:T(128)} %bitcast.60, s32[]{:T(128)} %bitcast.61, s32[]{:T(128)} %bitcast.62), kind=kLoop, calls=%fused_computation.clone.1.clone | loop fusion | bytes 8390656 | tf_op jit(solution)/shard_map/vmap()/gather
  180.9 14.9 %fusion.32 = f32[2,64,4096]{2,1,0:T(8,128)S(1)} fusion(f32[2,256,4096]{2,1,0:T(8,128)} %slice_subtract_fusion, f32[2,256,4096]{2,1,0:T(8,128)} %fusion.64, f32[2]{0:T(128)S(1)} %compare_convert_fusion, f32[64,256]{1,0:T(8,128)S(1)} %copy-done.3, f32[2,256,4096]{2,1,0:T(8,128)} %get-tuple-element.92, f32[2,264,4096]{2,1,0:T(8,128)} %fusion.7), kind=kOutput, calls=%fused_computation.53 | convolution fusion | flops 1625292800 | bytes 35717128 | tf_op jit(solution)/shard_map/nr,trc->tnc/dot_general | solution.py:109
  195.8 1.8 fusion.62
  197.6 12.7 %psum.28 = f32[2,64,64]{2,1,0:T(8,128)S(1)} all-reduce(f32[2,64,64]{2,1,0:T(8,128)S(1)} %fusion.62), channel_id=1, replica_groups=mesh['tilt'=8,'tile'=4] {'tile'}, use_global_device_ids=true, to_apply=%region_0.1 | all-reduce | flops 8192 | bytes 65536 | tf_op jit(solution)/shard_map/psum | solution.py:111
  210.3 0.3 convolution_bitcast_fusion.1
  210.6 0.1 multiply_reduce_fusion.1
  210.7 13.9 %fusion.15 = (f32[2]{0:T(128)S(1)}, f32[2,256,4096]{2,1,0:T(8,128)}) fusion(f32[2,256,4096]{2,1,0:T(8,128)} %fusion.64, f32[2,256,4096]{2,1,0:T(8,128)} %slice_subtract_fusion, f32[2]{0:T(128)S(1)} %compare_convert_fusion, f32[2,256,64]{1,2,0:T(8,128)S(1)} %convolution_bitcast_fusion.1, f32[64,4096]{1,0:T(8,128)S(1)} %copy-done), kind=kOutput, calls=%fused_computation.36 | convolution fusion | flops 1623195648 | bytes 26345488 | tf_op jit(solution)/shard_map/trm,mc->trc/dot_general | solution.py:114
  224.6 7.4 %psum.29 = f32[2]{0:T(128)S(1)} all-reduce(f32[2]{0:T(128)S(1)} %get-tuple-element.140), channel_id=1, replica_groups=mesh['tilt'=8,'tile'=4] {'tile'}, use_global_device_ids=true, to_apply=%region_3.4 | all-reduce | flops 2 | bytes 16 | tf_op jit(solution)/shard_map/psum | solution.py:116
  232.1 17.4 %fusion.29 = f32[2,64,4096]{2,1,0:T(8,128)S(1)} fusion(f32[2,256,4096]{2,1,0:T(8,128)} %get-tuple-element.141, f32[2,256,4096]{2,1,0:T(8,128)} %fusion.64, f32[2,256,4096]{2,1,0:T(8,128)} %slice_subtract_fusion, f32[2]{0:T(128)S(1)} %add_divide_fusion.1, f32[2]{0:T(128)S(1)} %compare_convert_fusion, f32[64,256]{1,0:T(8,128)S(1)} %copy-done.3, ...), kind=kOutput, calls=%fused_computation.52 | convolution fusion | flops 1629487104 | bytes 44105744 | tf_op jit(solution)/shard_map/nr,trc->tnc/dot_general | solution.py:109
  249.5 1.8 fusion.58
  251.3 11.2 %psum.30 = f32[2,64,64]{2,1,0:T(8,128)S(1)} all-reduce(f32[2,64,64]{2,1,0:T(8,128)S(1)} %fusion.58), channel_id=1, replica_groups=mesh['tilt'=8,'tile'=4] {'tile'}, use_global_device_ids=true, to_apply=%region_4.5 | all-reduce | flops 8192 | bytes 65536 | tf_op jit(solution)/shard_map/psum | solution.py:111
  262.5 0.3 convolution_bitcast_fusion
  262.8 12.2 %fusion.16 = f32[2]{0:T(128)S(1)} fusion(f32[2,256,4096]{2,1,0:T(8,128)} %fusion.64, f32[2,256,4096]{2,1,0:T(8,128)} %slice_subtract_fusion, f32[2,256,64]{1,2,0:T(8,128)S(1)} %convolution_bitcast_fusion, f32[2]{0:T(128)S(1)} %compare_convert_fusion, f32[64,4096]{1,0:T(8,128)S(1)} %copy-done), kind=kOutput, calls=%fused_computation.37 | convolution fusion | flops 1623195648 | bytes 17956880 | tf_op jit(solution)/shard_map/trm,mc->trc/dot_general | solution.py:114
  275.0 0.1 multiply_reduce_fusion
  275.1 5.7 %psum.31 = f32[2]{0:T(128)S(1)} all-reduce(f32[2]{0:T(128)S(1)} %fusion.16), channel_id=1, replica_groups=mesh['tilt'=8,'tile'=4] {'tile'}, use_global_device_ids=true, to_apply=%region_7.8 | all-reduce | flops 2 | bytes 16 | tf_op jit(solution)/shard_map/psum | solution.py:116
  280.9 0.1 fusion.85
  281.0 30.9 %all_gather.3 = f32[8,16,64]{2,1,0:T(8,128)S(1)} all-gather(f32[1,16,64]{2,1,0:T(8,128)S(1)} %slice.276), channel_id=1, replica_groups=mesh['tilt'=8,'tile'=4] {'tilt'}, dimensions={0}, use_global_device_ids=true | all-gather | bytes 36864 | tf_op jit(solution)/shard_map/all_gather | solution.py:37
  311.9 0.2 while.18
  312.1 0.7 subtract_add_fusion
  (28 shorter events, 0.2 us)
Async XLA Ops:
  0.0 195.8 %copy-start = (f32[64,4096]{1,0:T(8,128)S(1)}, f32[64,4096]{1,0:T(8,128)}, u32[]{:S(2)}) copy-start(f32[64,4096]{1,0:T(8,128)} %param.15) | copy-start | bytes 3145732
  0.0 11.1 %copy-start.4 = (f32[9]{0:T(128)S(1)}, f32[9]{0:T(128)}, u32[]{:S(2)}) copy-start(f32[9]{0:T(128)} %param.10) | copy-start | bytes 112
  1.2 10.6 %collective-permute-start = (f32[2,8,4096]{2,1,0:T(8,128)S(1)}, f32[2,8,4096]{2,1,0:T(8,128)S(1)}, u32[]{:S(2)}, u32[]{:S(2)}) collective-permute-start(f32[2,8,4096]{2,1,0:T(8,128)S(1)} %get-tuple-element.128), channel_id=1, source_target_pairs={{0,1},{1,2},{2,3},{4,5},{5,6},{6,7},{8,9},{9,10},{10,11},{12,13},{... | collective-permute-start | bytes 786440 | tf_op jit(solution)/shard_map/ppermute | solution.py:21
  3.6 12.2 %collective-permute-start.1 = (f32[2,8,4096]{2,1,0:T(8,128)S(1)}, f32[2,8,4096]{2,1,0:T(8,128)S(1)}, u32[]{:S(2)}, u32[]{:S(2)}) collective-permute-start(f32[2,8,4096]{2,1,0:T(8,128)S(1)} %get-tuple-element.127), channel_id=1, source_target_pairs={{1,0},{2,1},{3,2},{5,4},{6,5},{7,6},{9,8},{10,9},{11,10},{13,12},{... | collective-permute-start | bytes 786440 | tf_op jit(solution)/shard_map/ppermute | solution.py:24
  15.8 4.9 %copy-start.2 = (f32[2,272,4096]{2,1,0:T(8,128)}, f32[2,272,4096]{2,1,0:T(8,128)S(1)}, u32[]{:S(2)}) copy-start(f32[2,272,4096]{2,1,0:T(8,128)S(1)} %constant_dynamic-update-slice_fusion) | copy-start | bytes 26738692
  18.4 99.7 %collective-permute-start.2 = (f32[272,4096]{1,0:T(8,128)}, f32[272,4096]{1,0:T(8,128)}, u32[]{:S(2)}, u32[]{:S(2)}) collective-permute-start(f32[272,4096]{1,0:T(8,128)} %slice_bitcast_fusion), channel_id=1, source_target_pairs={{4,0},{8,4},{12,8},{16,12},{20,16},{24,20},{28,24},{5,1},{9,5},{13... | collective-permute-start | bytes 13369352 | tf_op jit(solution)/shard_map/ppermute | solution.py:32
  84.0 3.5 %copy-start.1 = (f32[2,264,4096]{2,1,0:T(8,128)S(1)}, f32[2,264,4096]{2,1,0:T(8,128)}, u32[]{:S(2)}) copy-start(f32[2,264,4096]{2,1,0:T(8,128)} %fusion.7) | copy-start | bytes 25952260
  146.7 11.7 %slice-start = ((f32[2,264,4096]{2,1,0:T(8,128)}), f32[1,264,4096]{2,1,0:T(8,128)S(1)}, s32[]{:S(2)}) async-start(f32[2,264,4096]{2,1,0:T(8,128)} %fusion.7), calls=%async_computation | async-start | bytes 8650752 | tf_op jit(solution)/shard_map/slice | solution.py:79
  165.1 15.7 %copy-start.3 = (f32[64,256]{1,0:T(8,128)S(1)}, f32[64,256]{1,0:T(8,128)}, u32[]{:S(2)}) copy-start(f32[64,256]{1,0:T(8,128)} %param.14) | copy-start | bytes 196612
where the time goes:
time: 316 us; the launch traced here: 313 us
  other arithmetic  119 us (38%)
  blocking collectives  68 us (22%)
  matrix products  67.9 us (21%)
  local copies, waits for them, and re-layouts  29.5 us (9%)
  waiting for transfers between devices  22.6 us (7%)
  starting transfers between devices  5.51 us (2%)
    add x2, other arithmetic, filter_columns(): total = total + taps[offset] * padded[..., offset:offset + columns]  75.9 us
    dot_general x2, matrix products, shards(): jnp.einsum('nr,trc->tnc', rows_interp, weighted, precision=highest)  32.3 us
    all_gather x1, blocking collectives, carried_in(): everything = lax.all_gather(value, axis)  30.9 us
    dot_general x2, matrix products, shards(): jnp.einsum('trm,mc->trc', row_part, cols_interp, precision=highest)  26.1 us
    psum x2, blocking collectives, shards(): grad = lax.psum(partial_grad, 'tile')  23.9 us
    ppermute x1, waiting for transfers between devices, shifted(): lax.ppermute(value, axis, [(source, source + steps) for source in range(i...  22.6 us
    mul x1, other arithmetic, shards(): filtered = filter_rows_valid(filter_columns(banded, taps), taps) * inside  16 us
    gather x6, local copies, waits for them, and re-layouts  15.7 us
  transfers between devices with their start and end apart: 3, of which 1 were waited for; matrix products, arithmetic and copies ran while one was open for 26% of the time, Pallas kernels for 0%

commit v1 on v0

v1 whole, which is shorter than its diff:
```python
import functools

import jax
import jax.numpy as jnp
from jax import lax
from jax.experimental import pallas as pl
from jax.experimental.pallas import tpu as pltpu
from jax.sharding import PartitionSpec as P

RAD = 4
SMAX = 4
PATCH_HALF = 256
MARGIN = RAD + SMAX
CHUNK = 64
COLB = 512
PAD = 128
epsilon = 1e-06
F32 = jnp.float32
BF16 = jnp.bfloat16
HI = lax.Precision.HIGHEST


def shifted(value, axis, steps):
    count = lax.axis_size(axis)
    initial, last = (max(0, -steps), min(count, count - steps))
    return lax.ppermute(value, axis, [(source, source + steps) for source in range(initial, last)])


def split_rows(x):
    hi = x.astype(BF16)
    lo = (x - hi.astype(F32)).astype(BF16)
    return jnp.concatenate([hi, lo, hi], axis=0)


def mm(a, b):
    return jnp.dot(a, b, preferred_element_type=F32)


def mm_hi(a, b):
    return lax.dot_general(
        a, b, (((1,), (0,)), ((), ())), precision=HI, preferred_element_type=F32
    )


def mm_hi_t(a, b):
    return lax.dot_general(
        a, b, (((1,), (1,)), ((), ())), precision=HI, preferred_element_type=F32
    )


def filter_strip(x, taps_ref, cols):
    xp = jnp.concatenate([x, jnp.zeros((x.shape[0], PAD), F32)], axis=1)
    width = cols + PAD
    total = taps_ref[RAD] * xp
    for k in range(2 * RAD + 1):
        if k != RAD:
            total = total + taps_ref[k] * pltpu.roll(xp, (RAD - k) % width, 1)
    return total


def band(taps_ref, dy):
    ext = CHUNK + 2 * MARGIN
    y = lax.broadcasted_iota(jnp.int32, (CHUNK, ext), 0)
    j = lax.broadcasted_iota(jnp.int32, (CHUNK, ext), 1)
    d = j - y - (MARGIN - RAD) - dy
    out = jnp.zeros((CHUNK, ext), F32)
    for k in range(2 * RAD + 1):
        out = jnp.where(d == k, taps_ref[k], out)
    return out


def split3(m):
    hi = m.astype(BF16)
    lo = (m - hi.astype(F32)).astype(BF16)
    return hi, lo


def k1(taps_ref, info_ref, prow_ref, pcol_ref, up_ref, main_ref, down_ref, rcat_ref,
       w_ref, w2_ref, left_ref, e_s, f_s, m_s, p_s, cb_s):
    rows, cols = main_ref.shape[1:]
    t = pl.program_id(0)
    band_start = info_ref[0]
    valid = info_ref[2 + 3 * t].astype(F32)
    e_s[0:8, :] = filter_strip(up_ref[0], taps_ref, cols)[:, :cols]
    e_s[rows + 8 : rows + 16, :] = filter_strip(down_ref[0], taps_ref, cols)[:, :cols]

    def strip(i, c):
        r = pl.multiple_of(i * 8, 8)
        e_s[pl.ds(r + 8, 8), :] = filter_strip(main_ref[0, pl.ds(r, 8), :], taps_ref, cols)[:, :cols]
        return c

    lax.fori_loop(0, rows // 8, strip, 0)
    left_ref[...] = jnp.zeros_like(left_ref)
    patches = prow_ref.shape[2]
    xcol = lax.broadcasted_iota(jnp.int32, (patches, cols), 1)
    cb_s[...] = (jnp.abs(xcol - pcol_ref[0]) <= PATCH_HALF).astype(F32).astype(BF16)
    tm_hi, tm_lo = split3(band(taps_ref, 0))

    def chunk(c, carry):
        base = pl.multiple_of(c * CHUNK, CHUNK)
        yrow = band_start + base + lax.broadcasted_iota(jnp.int32, (CHUNK, patches), 0)
        rb = ((jnp.abs(yrow - prow_ref[0]) <= PATCH_HALF).astype(F32) * valid).astype(BF16)
        for b in range(cols // COLB):
            cs = slice(b * COLB, (b + 1) * COLB)
            e = e_s[pl.ds(base, CHUNK + 2 * MARGIN), cs]
            eh, el = split3(e)
            f_s[:, cs] = mm(tm_hi, eh) + (mm(tm_hi, el) + mm(tm_lo, eh))
            m_s[:, cs] = mm(rb, cb_s[:, cs])

        def weigh(i, cc):
            r = pl.multiple_of(i * 8, 8)
            f = f_s[pl.ds(r, 8), :]
            fp = jnp.concatenate([f, jnp.zeros((8, PAD), F32)], axis=1)
            wd = cols + PAD
            gx = 0.5 * (pltpu.roll(fp, wd - 1, 1) - pltpu.roll(fp, 1, 1))[:, :cols]
            w = m_s[pl.ds(r, 8), :] * gx
            ro = pl.multiple_of(base + r, 8)
            w_ref[0, pl.ds(ro, 8), :] = w
            w2_ref[0, pl.ds(ro, 8), :] = w * gx
            p_s[pl.ds(r, 8), :] = w * f
            return cc

        lax.fori_loop(0, CHUNK // 8, weigh, 0)
        rc = rcat_ref[c]
        for b in range(cols // COLB):
            cs = slice(b * COLB, (b + 1) * COLB)
            left_ref[0, :, cs] += mm(rc, split_rows(p_s[:, cs]))
        return carry

    lax.fori_loop(0, rows // CHUNK, chunk, 0)


def k2(taps_ref, info_ref, up_ref, main_ref, down_ref, rcat_ref, w_ref, left_ref, e_s, *, first):
    rows, cols = main_ref.shape[1:]
    t = pl.program_id(0) + first
    band_start = info_ref[0]
    total_rows = info_ref[1]
    dy = info_ref[3 + 3 * t]
    dx = info_ref[4 + 3 * t]
    wd = cols + PAD
    turn = lax.rem(wd - dx, wd)
    x = lax.broadcasted_iota(jnp.int32, (8, cols), 1) + dx
    inside = (x >= 0) & (x < cols)

    def place(v):
        e = pltpu.roll(filter_strip(v, taps_ref, cols), turn, 1)[:, :cols]
        return jnp.where(inside, e, 0.0)

    e_s[0:8, :] = place(up_ref[0])
    e_s[rows + 8 : rows + 16, :] = place(down_ref[0])

    def strip(i, c):
        r = pl.multiple_of(i * 8, 8)
        e_s[pl.ds(r + 8, 8), :] = place(main_ref[0, pl.ds(r, 8), :])
        return c

    lax.fori_loop(0, rows // 8, strip, 0)
    left_ref[...] = jnp.zeros_like(left_ref)
    tm = band(taps_ref, dy)
    yl = lax.broadcasted_iota(jnp.int32, tm.shape, 0) + band_start + dy

    def chunk(c, carry):
        base = pl.multiple_of(c * CHUNK, CHUNK)
        y = yl + base
        tm_hi, tm_lo = split3(jnp.where((y >= 0) & (y < total_rows), tm, 0.0))
        rc = rcat_ref[c]
        for b in range(cols // COLB):
            cs = slice(b * COLB, (b + 1) * COLB)
            eh, el = split3(e_s[pl.ds(base, CHUNK + 2 * MARGIN), cs])
            q = mm(tm_hi, eh) + (mm(tm_hi, el) + mm(tm_lo, eh))
            p = w_ref[0, pl.ds(base, CHUNK), cs] * q
            left_ref[0, :, cs] += mm(rc, split_rows(p))
        return carry

    lax.fori_loop(0, rows // CHUNK, chunk, 0)


def refine(*refs, n, final, sizes):
    if final:
        (lq_ref, lf_ref, w2_ref, c_ref, ccat_ref, rt_ref, rcat_ref, sel_ref, gl_ref, out_ref,
         left_s, cat_s, acc_s, send_s, slots, csend_s, cslots, ssem, rsem, csem, crsem) = refs
    else:
        (lq_ref, lf_ref, w2_ref, c_ref, ccat_ref, rt_ref, rcat_ref, sel_ref, out_ref,
         left_s, cat_s, acc_s, send_s, slots, ssem, rsem) = refs
    tiles, tilts = sizes
    nodes, cols = c_ref.shape
    rows = rt_ref.shape[0]
    me = lax.axis_index("tile")
    place = lax.axis_index("tilt")
    barrier = pltpu.get_barrier_semaphore()
    for d in range(1, tiles):
        pl.semaphore_signal(barrier, inc=1, device_id={"tile": lax.rem(me + d, tiles)})
    waits = tiles - 1
    if final:
        for d in range(1, tilts):
            pl.semaphore_signal(barrier, inc=1, device_id={"tilt": lax.rem(place + d, tilts)})
        waits += tilts - 1
    pl.semaphore_wait(barrier, waits)

    def exchange(rnd):
        copies = []
        for d in range(1, tiles):
            copies.append(pltpu.make_async_remote_copy(
                src_ref=send_s.at[rnd], dst_ref=slots.at[rnd, me],
                send_sem=ssem.at[rnd, d - 1], recv_sem=rsem.at[rnd, d - 1],
                device_id={"tile": lax.rem(me + d, tiles)}))
        for cp in copies:
            cp.start()
        slots[rnd, me] = send_s[rnd]
        for cp in copies:
            cp.wait()
        total = slots[rnd, 0]
        for k in range(1, tiles):
            total = total + slots[rnd, k]
        return total

    def direction(g, w2, apply):
        g3 = mm_hi(mm_hi(rt_ref[...], g), sel_ref[...])
        hi, lo = split3(g3)
        lane = lax.broadcasted_iota(jnp.int32, g3.shape, 1)
        cat_s[...] = jnp.where(lane < 2 * nodes, hi.astype(F32), lo.astype(F32)).astype(BF16)
        acc_s[...] = jnp.zeros_like(acc_s)
        if apply:
            left_s[...] = jnp.zeros_like(left_s)

        def chunk(c, carry):
            base = pl.multiple_of(c * CHUNK, CHUNK)
            gc = cat_s[pl.ds(base, CHUNK), :]
            rc = rcat_ref[c]
            for b in range(cols // COLB):
                cs = slice(b * COLB, (b + 1) * COLB)
                v = mm(gc, ccat_ref[:, cs])
                y = w2_ref[w2, pl.ds(base, CHUNK), cs] * v
                acc_s[...] += y * v
                if apply:
                    left_s[:, cs] += mm(rc, split_rows(y))
            return carry

        lax.fori_loop(0, rows // CHUNK, chunk, 0)
        return jnp.sum(acc_s[...])

    grids = []
    for s in range(n):
        r = 3 * s
        send_s[r] = jnp.zeros_like(send_s[r])
        send_s[r, :nodes, :nodes] = mm_hi_t(lq_ref[s] - lf_ref[s], c_ref[...])
        g1 = exchange(r)[:nodes, :nodes]
        gg1 = jnp.sum(g1 * g1)
        jj1 = direction(g1, s, True)
        send_s[r + 1] = jnp.zeros_like(send_s[r + 1])
        send_s[r + 1, :nodes, :nodes] = mm_hi_t(left_s[...], c_ref[...])
        send_s[r + 1, nodes : nodes + 8, :] = jnp.full((8, send_s.shape[2]), jj1, F32)
        both = exchange(r + 1)
        h1 = both[:nodes, :nodes]
        jj1 = jnp.sum(both[nodes : nodes + 1, 0:1])
        a1 = jnp.full((nodes, nodes), gg1, F32) / jnp.full((nodes, nodes), jj1 + epsilon, F32)
        g2 = g1 - a1 * h1
        gg2 = jnp.sum(g2 * g2)
        jj2 = direction(g2, s, False)
        send_s[r + 2] = jnp.full(send_s.shape[1:], jj2, F32)
        jj2 = jnp.sum(exchange(r + 2)[0:1, 0:1])
        a2 = jnp.full((nodes, nodes), gg2, F32) / jnp.full((nodes, nodes), jj2 + epsilon, F32)
        grids.append(-(a1 * g1) - a2 * g2)
    if not final:
        for s in range(n):
            out_ref[s] = grids[s]
        return
    share = nodes // tiles
    send_rows = csend_s.shape[0]
    row = lax.broadcasted_iota(jnp.int32, (send_rows, nodes), 0) + me * share
    pick = (row == lax.broadcasted_iota(jnp.int32, (send_rows, nodes), 1)).astype(F32)
    run = jnp.zeros((nodes, nodes), F32)
    count = out_ref.shape[0]
    stack = [gl_ref[i] for i in range(count - n)] + grids
    parts = []
    for i in range(count):
        parts.append(mm_hi(pick, run))
        run = run + stack[i]
    csend_s[...] = jnp.zeros_like(csend_s)
    csend_s[:, :nodes] = mm_hi(pick, run)
    copies = []
    for d in range(1, tilts):
        copies.append(pltpu.make_async_remote_copy(
            src_ref=csend_s, dst_ref=cslots.at[place],
            send_sem=csem.at[d - 1], recv_sem=crsem.at[d - 1],
            device_id={"tilt": lax.rem(place + d, tilts)}))
    for cp in copies:
        cp.start()
    cslots[place] = csend_s[...]
    for cp in copies:
        cp.wait()
    before = jnp.zeros((send_rows, 128), F32)
    for k in range(tilts):
        before = before + jnp.where(k < place, cslots[k], 0.0)
    for i in range(count):
        out_ref[i] = (before[:, :nodes] + parts[i])[:share]


def shards(images, taps, shifts, patch_rows, patch_cols, rows_interp, cols_interp):
    tilt_count, rows, cols = images.shape
    tiles, tilts = lax.axis_size("tile"), lax.axis_size("tilt")
    nodes = cols_interp.shape[0]
    patches = patch_rows.shape[1]
    raw_next = shifted(images[0], "tilt", -1)
    low = shifted(images[:, rows - MARGIN :, :], "tile", 1)
    high = shifted(images[:, :MARGIN, :], "tile", -1)
    rim = shifted(jnp.concatenate([low[0], high[0]], axis=0), "tilt", -1)

    t_global = lax.axis_index("tilt") * tilt_count + jnp.arange(tilt_count, dtype=jnp.int32)
    valid = (t_global < tilt_count * tilts - 1).astype(jnp.int32)
    head = jnp.stack([lax.axis_index("tile") * rows, jnp.int32(rows * tiles)]).astype(jnp.int32)
    info = jnp.concatenate([head, jnp.concatenate([valid[:, None], shifts], axis=1).reshape(-1)])

    def halves(x):
        hi = lax.reduce_precision(x, 8, 7)
        return hi.astype(BF16), (x - hi).astype(BF16)

    chunks = rows // CHUNK
    rh, rl = halves(rows_interp.reshape(nodes, chunks, CHUNK).transpose(1, 0, 2))
    rcat = jnp.concatenate([rh, rh, rl], axis=2)
    ch, cl = halves(cols_interp)
    ccat = jnp.concatenate([ch, cl, ch], axis=0)
    eye = jnp.eye(nodes, dtype=F32)
    sel = jnp.concatenate([eye, eye, eye], axis=1)

    smem = pl.BlockSpec(memory_space=pltpu.SMEM)
    vmem = pl.BlockSpec(memory_space=pltpu.VMEM)
    vm = 60 << 20

    def per(shape, off=0):
        return pl.BlockSpec((1,) + shape, lambda i: (i + off, 0, 0))

    def whole(shape):
        return pl.BlockSpec(shape, lambda i: (0,) * len(shape))

    e_scratch = pltpu.VMEM((rows + 2 * MARGIN, cols), F32)
    big = rows * cols
    w, w2, left_f = pl.pallas_call(
        k1,
        grid=(tilt_count,),
        in_specs=[smem, smem, per((1, patches)), per((patches, 1)), per((MARGIN, cols)),
                  per((rows, cols)), per((MARGIN, cols)), whole(rcat.shape)],
        out_specs=[per((rows, cols)), per((rows, cols)), per((nodes, cols))],
        out_shape=[jax.ShapeDtypeStruct((tilt_count, rows, cols), F32),
                   jax.ShapeDtypeStruct((tilt_count, rows, cols), F32),
                   jax.ShapeDtypeStruct((tilt_count, nodes, cols), F32)],
        scratch_shapes=[e_scratch, pltpu.VMEM((CHUNK, cols), F32), pltpu.VMEM((CHUNK, cols), F32),
                        pltpu.VMEM((CHUNK, cols), F32), pltpu.VMEM((patches, cols), BF16)],
        compiler_params=pltpu.CompilerParams(vmem_limit_bytes=vm),
        cost_estimate=pl.CostEstimate(flops=60 * big * tilt_count, bytes_accessed=40 * big * tilt_count,
                                      transcendentals=0),
        name="weigh",
    )(taps, info, patch_rows[:, None, :], patch_cols[:, :, None], low, images, high, rcat)

    def partner(up, main, down, first, count, off):
        return pl.pallas_call(
            functools.partial(k2, first=first),
            grid=(count,),
            in_specs=[smem, smem, per((MARGIN, cols), off), per((rows, cols), off),
                      per((MARGIN, cols), off), whole(rcat.shape), per((rows, cols), first)],
            out_specs=per((nodes, cols)),
            out_shape=jax.ShapeDtypeStruct((count, nodes, cols), F32),
            scratch_shapes=[e_scratch],
            compiler_params=pltpu.CompilerParams(vmem_limit_bytes=vm),
            cost_estimate=pl.CostEstimate(flops=40 * big * count, bytes_accessed=30 * big * count,
                                          transcendentals=0),
            name="partner",
        )(taps, info, up, main, down, rcat, w)

    rt = rows_interp.T

    def step(lq, lf, w2s, final, cid, extra=()):
        n = lq.shape[0]
        scratch = [pltpu.VMEM((nodes, cols), F32), pltpu.VMEM((rows, 3 * nodes), BF16),
                   pltpu.VMEM((CHUNK, COLB), F32), pltpu.VMEM((3 * n, nodes + 8, 128), F32),
                   pltpu.VMEM((3 * n, tiles, nodes + 8, 128), F32)]
        sems = [pltpu.SemaphoreType.DMA((3 * n, tiles - 1)), pltpu.SemaphoreType.DMA((3 * n, tiles - 1))]
        if final:
            share = nodes // tiles
            wide = max(8, share)
            scratch += [pltpu.VMEM((wide, 128), F32), pltpu.VMEM((tilts, wide, 128), F32)]
            sems += [pltpu.SemaphoreType.DMA((tilts - 1,)), pltpu.SemaphoreType.DMA((tilts - 1,))]
            out = jax.ShapeDtypeStruct((tilt_count, share, nodes), F32)
        else:
            out = jax.ShapeDtypeStruct((n, nodes, nodes), F32)
        off = tilt_count - 1 if final else 0
        args = (lq, lf, w2s, cols_interp, ccat, rt, rcat, sel) + tuple(extra)
        specs = [whole(lq.shape), pl.BlockSpec((n,) + lf.shape[1:], lambda i: (off, 0, 0)),
                 pl.BlockSpec((n,) + w2s.shape[1:], lambda i: (off, 0, 0))]
        specs += [whole(a.shape) for a in args[3:]]
        return pl.pallas_call(
            functools.partial(refine, n=n, final=final, sizes=(tiles, tilts)),
            grid=(1,),
            in_specs=specs,
            out_specs=pl.BlockSpec(out.shape, lambda i: (0, 0, 0)),
            out_shape=out,
            scratch_shapes=scratch + sems,
            compiler_params=pltpu.CompilerParams(
                collective_id=cid, has_side_effects=True, vmem_limit_bytes=vm),
            cost_estimate=pl.CostEstimate(flops=60 * big, bytes_accessed=40 * big, transcendentals=0),
            name="refine_last" if final else "refine_local",
        )(*args)

    local = tilt_count - 1
    extra = ()
    if local:
        lq = partner(low, images, high, 0, local, 1)
        extra = (step(lq, left_f, w2, False, 1),)
    else:
        extra = (jnp.zeros((1, nodes, nodes), F32),)
    lq_last = partner(rim[None, :MARGIN], raw_next[None], rim[None, MARGIN:], tilt_count - 1, 1, 0)
    return step(lq_last, left_f, w2, True, 2, extra)


def solution(mesh):
    return jax.shard_map(
        shards,
        mesh=mesh,
        in_specs=(
            P("tilt", "tile", None),
            P(),
            P("tilt", None),
            P("tilt", None),
            P("tilt", None),
            P(None, "tile"),
            P(),
        ),
        out_specs=P("tilt", "tile", None),
        check_vma=False,
    )
```

time: 316 us -> 194 us (0.61)
  Pallas kernels: 0 us -> 173 us
  other arithmetic: 119 us -> 3.65 us
  blocking collectives: 68 us -> 0 us
  matrix products: 67.9 us -> 0 us
  waiting for transfers between devices: 22.6 us -> 0.01 us
  local copies, waits for them, and re-layouts: 29.5 us -> 9.44 us
    pallas_call x0 -> x5, Pallas kernels: none -> 173 us  [the longest x2 67.6 us: step(): pl.pallas_call(functools.partial(refine, n=n, final=final, sizes=(tiles,...]
    add x4 -> x0, other arithmetic: 76.6 us -> none  [the longest x2 75.9 us: filter_columns(): total = total + taps[offset] * padded[..., offset:offset + columns]]
    dot_general x9 -> x0, matrix products: 67.9 us -> none  [the longest x2 32.3 us: shards(): jnp.einsum('nr,trc->tnc', rows_interp, weighted, precision=highest)]
    psum x4 -> x0, blocking collectives: 37 us -> none  [the longest x2 23.9 us: shards(): grad = lax.psum(partial_grad, 'tile')]
    all_gather x1 -> x0, blocking collectives: 30.9 us -> none  [carried_in(): everything = lax.all_gather(value, axis)]
    ppermute x1 -> x4, waiting for transfers between devices: 22.6 us -> 0.01 us  [shifted(): lax.ppermute(value, axis, [(source, source + steps) for source in range(i...]
    mul x1 -> x0, other arithmetic: 16 us -> none  [shards(): filtered = filter_rows_valid(filter_columns(banded, taps), taps) * inside]
    gather x6 -> x0, local copies, waits for them, and re-layouts: 15.7 us -> none
  transfers between devices with their start and end apart: 3 -> 4, of which waited for: 1 -> 0; matrix products, arithmetic and copies ran while one was open for 26% -> 6% of each run, Pallas kernels for 0% -> 55%
where the time goes in v1:
time: 194 us; the launch traced here: 193 us
  Pallas kernels  173 us (89%)
  local copies, waits for them, and re-layouts  9.44 us (5%)
  starting transfers between devices  7.17 us (4%)
  other arithmetic  3.65 us (2%)
    pallas_call x2, Pallas kernels, step(): pl.pallas_call(functools.partial(refine, n=n, final=final, sizes=(tiles,...  67.6 us
    pallas_call x2, Pallas kernels, partner(): pl.pallas_call(functools.partial(k2, first=first), grid=(count,), in_spec...  57 us
    pallas_call x1, Pallas kernels, shards(): pl.pallas_call(k1, grid=(tilt_count,), in_specs=[smem, smem, per((1, patc...  48.2 us
    ppermute x4, starting transfers between devices, shifted(): lax.ppermute(value, axis, [(source, source + steps) for source in range(i...  7.17 us
    squeeze x1, local copies, waits for them, and re-layouts, shards(): raw_next = shifted(images[0], 'tilt', -1)  4.61 us
  transfers between devices with their start and end apart: 4, of which 0 were waited for; matrix products, arithmetic and copies ran while one was open for 6% of the time, Pallas kernels for 55%

profile of v1, /device:TPU:0, one launch (start us, length us, event | category | flops | bytes accessed | tf_op | source)
XLA Modules:
  0.0 193.3 jit_solution(6800298535389734509)
XLA Ops:
  0.0 1.1 fusion.2
  1.1 1.3 collective-permute-start.1
  2.4 0.0 copy-start
  2.4 3.2 %collective-permute-start = (f32[2,8,4096]{2,1,0:T(8,128)S(1)}, f32[2,8,4096]{2,1,0:T(8,128)S(1)}, u32[]{:S(2)}, u32[]{:S(2)}) collective-permute-start(f32[2,8,4096]{2,1,0:T(8,128)S(1)} %get-tuple-element.11), channel_id=1, source_target_pairs={{0,1},{1,2},{2,3},{4,5},{5,6},{6,7},{8,9},{9,10},{10,11},{12,13},{... | collective-permute-start | bytes 786440 | tf_op jit(solution)/shard_map/ppermute | solution.py:26
  5.6 4.6 %slice_bitcast_fusion = f32[256,4096]{1,0:T(8,128)} fusion(f32[2,256,4096]{2,1,0:T(8,128)} %main_ref.3), kind=kLoop, calls=%fused_computation | loop fusion | bytes 8388608 | tf_op jit(solution)/shard_map/squeeze | solution.py:304
  10.2 0.0 copy-start.4
  10.2 0.0 copy-start.3
  10.2 1.4 collective-permute-start.3
  11.6 0.0 copy-done
  11.7 0.0 copy-start.5
  11.7 0.2 fusion
  11.8 1.3 pad_maximum_fusion.refs_4_
  13.1 0.0 copy-done.4
  13.2 0.1 pad_add_fusion
  13.2 0.1 reshape.19
  13.3 0.0 copy-done.3
  13.3 0.1 reshape.20
  13.5 0.0 collective-permute-done.1.down_ref
  13.5 0.0 copy-start.1
  13.5 0.0 collective-permute-done.up_ref
  13.5 0.0 copy-start.2
  13.6 1.3 collective-permute-start.2
  14.9 0.6 pad_add_fusion.1.info_ref
  15.5 0.8 copy.14
  16.2 0.0 copy-done.5
  16.2 0.7 copy.13.pcol_ref
  16.9 0.7 add_convert_fusion.refs_7_
  17.6 0.7 pad_maximum_fusion.2.rcat_ref.refs_6_
  18.4 0.0 copy-done.1
  18.4 0.0 copy-done.2
  18.4 48.2 %weigh.1 = (f32[2,256,4096]{2,1,0:T(8,128)}, f32[2,256,4096]{2,1,0:T(8,128)}, f32[2,64,4096]{2,1,0:T(8,128)}) custom-call(f32[9]{0:T(128)} %taps_ref.5, s32[8]{0:T(128)} %pad_add_fusion.1.info_ref, s32[2,1,16]{2,1,0:T(1,128)} %bitcast.22, s32[2,16,1]{2,1,0:T(8,128)} %copy.13.pcol_ref, f32[2,8,4096]{2,1,0:T(8,128)} %copy-done.2, f32[2,256,4096]{2,1,0:T(8,128)} %main_ref.3, ...), custom_call_target="tpu_custom_call" | custom-call | flops 125829120 | bytes 83886080 | tf_op jit(solution)/shard_map/weigh/pallas_call | solution.py:338
  66.6 28.5 %partner.3.refs_0_ = f32[1,64,4096]{2,1,0:T(8,128)} custom-call(f32[9]{0:T(128)} %taps_ref.5, s32[8]{0:T(128)} %pad_add_fusion.1.info_ref, f32[2,8,4096]{2,1,0:T(8,128)} %copy-done.2, f32[2,256,4096]{2,1,0:T(8,128)} %main_ref.3, f32[2,8,4096]{2,1,0:T(8,128)} %copy-done.1, bf16[4,64,192]{2,1,0:T(8,128)(2,1)} %pad_maximum_fusion.2.rcat_ref.refs_6_, ...), custom_call_target="tpu_custom_call" | custom-call | flops 41943040 | bytes 31457280 | tf_op jit(solution)/shard_map/partner/pallas_call | solution.py:356
  95.1 30.2 %refine_local.1.refs_8_ = f32[1,64,64]{2,1,0:T(8,128)} custom-call(f32[1,64,4096]{2,1,0:T(8,128)} %partner.3.refs_0_, f32[2,64,4096]{2,1,0:T(8,128)} %get-tuple-element.9.refs_1_, f32[2,256,4096]{2,1,0:T(8,128)} %get-tuple-element.10.refs_2_, f32[64,4096]{1,0:T(8,128)} %refs_3_.3, bf16[192,4096]{1,0:T(8,128)(2,1)} %pad_maximum_fusion.refs_4_, ...), custom_call_target="tpu_custom_call" | custom-call | flops 62914560 | bytes 41943040 | tf_op jit(solution)/shard_map/refine_local/pallas_call | solution.py:391
  125.3 0.0 collective-permute-done.2
  125.4 0.7 slice_bitcast_fusion.1
  126.1 0.0 collective-permute-done.3
  126.1 28.5 %partner.2.refs_0_ = f32[1,64,4096]{2,1,0:T(8,128)} custom-call(f32[9]{0:T(128)} %taps_ref.5, s32[8]{0:T(128)} %pad_add_fusion.1.info_ref, f32[1,8,4096]{2,1,0:T(8,128)} %get-tuple-element.16.up_ref, f32[1,256,4096]{2,1,0:T(8,128)} %bitcast.5.main_ref, f32[1,8,4096]{2,1,0:T(8,128)} %get-tuple-element.15.down_ref, ...), custom_call_target="tpu_custom_call" | custom-call | flops 41943040 | bytes 31457280 | tf_op jit(solution)/shard_map/partner/pallas_call | solution.py:356
  154.6 37.3 %refine_last.1 = f32[2,16,64]{2,1,0:T(8,128)} custom-call(f32[1,64,4096]{2,1,0:T(8,128)} %partner.2.refs_0_, f32[2,64,4096]{2,1,0:T(8,128)} %get-tuple-element.9.refs_1_, f32[2,256,4096]{2,1,0:T(8,128)} %get-tuple-element.10.refs_2_, f32[64,4096]{1,0:T(8,128)} %refs_3_.3, bf16[192,4096]{1,0:T(8,128)(2,1)} %pad_maximum_fusion.refs_4_, f32[256,64]{1,0:T(8,128)} %bitcast.21, ...), custom_call_target="tpu_custom_call" | custom-call | flops 62914560 | bytes 41943040 | tf_op jit(solution)/shard_map/refine_last/pallas_call | solution.py:391
  191.9 1.3 copy.18
  (6 shorter events, 0.1 us)
Async XLA Ops:
  1.1 12.4 %collective-permute-start.1 = (f32[2,8,4096]{2,1,0:T(8,128)S(1)}, f32[2,8,4096]{2,1,0:T(8,128)S(1)}, u32[]{:S(2)}, u32[]{:S(2)}) collective-permute-start(f32[2,8,4096]{2,1,0:T(8,128)S(1)} %get-tuple-element.12), channel_id=1, source_target_pairs={{1,0},{2,1},{3,2},{5,4},{6,5},{7,6},{9,8},{10,9},{11,10},{13,12},{... | collective-permute-start | bytes 786440 | tf_op jit(solution)/shard_map/ppermute | solution.py:26
  2.4 9.3 %copy-start = (f32[64,4096]{1,0:T(8,128)S(1)}, f32[64,4096]{1,0:T(8,128)}, u32[]{:S(2)}) copy-start(f32[64,4096]{1,0:T(8,128)} %refs_3_.3) | copy-start | bytes 3145732
  2.4 11.1 %collective-permute-start = (f32[2,8,4096]{2,1,0:T(8,128)S(1)}, f32[2,8,4096]{2,1,0:T(8,128)S(1)}, u32[]{:S(2)}, u32[]{:S(2)}) collective-permute-start(f32[2,8,4096]{2,1,0:T(8,128)S(1)} %get-tuple-element.11), channel_id=1, source_target_pairs={{0,1},{1,2},{2,3},{4,5},{5,6},{6,7},{8,9},{9,10},{10,11},{12,13},{... | collective-permute-start | bytes 786440 | tf_op jit(solution)/shard_map/ppermute | solution.py:26
  10.2 3.0 %copy-start.4 = (s32[2,2]{1,0:T(2,128)S(1)}, s32[2,2]{1,0:T(2,128)}, u32[]{:S(2)}) copy-start(s32[2,2]{1,0:T(2,128)} %param.9) | copy-start | bytes 52
  10.2 3.1 %copy-start.3 = (f32[64,256]{1,0:T(8,128)S(1)}, f32[64,256]{1,0:T(8,128)}, u32[]{:S(2)}) copy-start(f32[64,256]{1,0:T(8,128)} %param.12) | copy-start | bytes 196612
  10.2 115.9 %collective-permute-start.3 = (f32[256,4096]{1,0:T(8,128)}, f32[256,4096]{1,0:T(8,128)}, u32[]{:S(2)}, u32[]{:S(2)}) collective-permute-start(f32[256,4096]{1,0:T(8,128)} %slice_bitcast_fusion), channel_id=1, source_target_pairs={{4,0},{8,4},{12,8},{16,12},{20,16},{24,20},{28,24},{5,1},{9,5},{13... | collective-permute-start | bytes 12582920 | tf_op jit(solution)/shard_map/ppermute | solution.py:26
  11.7 4.6 %copy-start.5 = (s32[2,16]{1,0:T(2,128)S(1)}, s32[2,16]{1,0:T(2,128)}, u32[]{:S(2)}) copy-start(s32[2,16]{1,0:T(2,128)} %param.11) | copy-start | bytes 388
  13.5 4.9 %copy-start.1 = (f32[2,8,4096]{2,1,0:T(8,128)}, f32[2,8,4096]{2,1,0:T(8,128)S(1)}, u32[]{:S(2)}) copy-start(f32[2,8,4096]{2,1,0:T(8,128)S(1)} %collective-permute-done.1.down_ref) | copy-start | bytes 786436
  13.5 4.9 %copy-start.2 = (f32[2,8,4096]{2,1,0:T(8,128)}, f32[2,8,4096]{2,1,0:T(8,128)S(1)}, u32[]{:S(2)}) copy-start(f32[2,8,4096]{2,1,0:T(8,128)S(1)} %collective-permute-done.up_ref) | copy-start | bytes 786436
  13.6 111.8 %collective-permute-start.2 = (f32[16,4096]{1,0:T(8,128)S(1)}, f32[16,4096]{1,0:T(8,128)S(1)}, u32[]{:S(2)}, u32[]{:S(2)}) collective-permute-start(f32[16,4096]{1,0:T(8,128)S(1)} %pad_maximum_fusion.1), channel_id=1, source_target_pairs={{4,0},{8,4},{12,8},{16,12},{20,16},{24,20},{28,24},{5,1},{9,5},{13... | collective-permute-start | bytes 786440 | tf_op jit(solution)/shard_map/ppermute | solution.py:26

commit v2 on v1

--- a/solution.py
+++ b/solution.py
@@ -13,6 +13,8 @@
 MARGIN = RAD + SMAX
 CHUNK = 64
 COLB = 512
+WIDE = 256
+GROUP = 32
 PAD = 128
 epsilon = 1e-06
 F32 = jnp.float32
@@ -48,14 +50,80 @@
     )
 
 
-def filter_strip(x, taps_ref, cols):
-    xp = jnp.concatenate([x, jnp.zeros((x.shape[0], PAD), F32)], axis=1)
-    width = cols + PAD
-    total = taps_ref[RAD] * xp
+def toeplitz(taps_ref, dx, th_s, tl_s):
+    i = lax.broadcasted_iota(jnp.int32, (2 * WIDE, WIDE), 0)
+    o = lax.broadcasted_iota(jnp.int32, (2 * WIDE, WIDE), 1)
+    rel = jnp.where(i < WIDE, i, jnp.where(i < WIDE + PAD, i - WIDE - PAD, i - PAD))
+    d = rel - o - dx + RAD
+    t = jnp.zeros((2 * WIDE, WIDE), F32)
     for k in range(2 * RAD + 1):
-        if k != RAD:
-            total = total + taps_ref[k] * pltpu.roll(xp, (RAD - k) % width, 1)
-    return total
+        t = jnp.where(d == k, taps_ref[k], t)
+    th_s[...], tl_s[...] = split3(t)
+
+
+def filter_group(load, store, rows, cols, dx, th_s, tl_s):
+    blocks = cols // PAD
+    zero = jnp.zeros((rows, PAD), BF16)
+    his, los = [zero], [zero]
+    for b in range(blocks):
+        hi, lo = split3(load(b * PAD, PAD))
+        his.append(hi)
+        los.append(lo)
+    his.append(zero)
+    los.append(zero)
+
+    def gather(v):
+        return jnp.concatenate(
+            [jnp.concatenate([v[2 * b + 1], v[2 * b + 2], v[2 * b], v[2 * b + 3]], axis=1)
+             for b in range(blocks // 2)], axis=0)
+
+    xh, xl = gather(his), gather(los)
+    th = th_s[...]
+    e = mm(xh, th) + (mm(xl, th) + mm(xh, tl_s[...]))
+    for b in range(blocks // 2):
+        v = e[b * rows : (b + 1) * rows]
+        if b == 0 or b == blocks // 2 - 1:
+            x = lax.broadcasted_iota(jnp.int32, v.shape, 1) + (b * WIDE + dx)
+            v = jnp.where((x >= 0) & (x < cols), v, 0.0)
+        store(b * WIDE, v)
+
+
+def filter_pieces(pieces, e_s, cols, dx, th_s, tl_s):
+    at = 0
+    for ref in pieces:
+        m = ref.shape[1]
+        groups = m // GROUP
+
+        def body(i, carry, ref=ref, at=at):
+            r = pl.multiple_of(i * GROUP, 8)
+            ro = pl.multiple_of(i * GROUP + at, 8)
+
+            def load(c, w):
+                return ref[0, pl.ds(r, GROUP), c : c + w]
+
+            def store(c, v):
+                e_s[pl.ds(ro, GROUP), c : c + WIDE] = v
+
+            filter_group(load, store, GROUP, cols, dx, th_s, tl_s)
+            return carry
+
+        if groups:
+            lax.fori_loop(0, groups, body, 0)
+        done = groups * GROUP
+        left = m - done
+        while left:
+            size = 16 if left >= 16 else 8
+
+            def load(c, w, ref=ref, done=done, size=size):
+                return ref[0, done : done + size, c : c + w]
+
+            def store(c, v, at=at, done=done, size=size):
+                e_s[at + done : at + done + size, c : c + WIDE] = v
+
+            filter_group(load, store, size, cols, dx, th_s, tl_s)
+            done += size
+            left -= size
+        at += m
 
 
 def band(taps_ref, dy):
@@ -76,20 +144,13 @@
 
 
 def k1(taps_ref, info_ref, prow_ref, pcol_ref, up_ref, main_ref, down_ref, rcat_ref,
-       w_ref, w2_ref, left_ref, e_s, f_s, m_s, p_s, cb_s):
+       w_ref, w2_ref, left_ref, e_s, f_s, m_s, p_s, cb_s, th_s, tl_s):
     rows, cols = main_ref.shape[1:]
     t = pl.program_id(0)
     band_start = info_ref[0]
     valid = info_ref[2 + 3 * t].astype(F32)
-    e_s[0:8, :] = filter_strip(up_ref[0], taps_ref, cols)[:, :cols]
-    e_s[rows + 8 : rows + 16, :] = filter_strip(down_ref[0], taps_ref, cols)[:, :cols]
-
-    def strip(i, c):
-        r = pl.multiple_of(i * 8, 8)
-        e_s[pl.ds(r + 8, 8), :] = filter_strip(main_ref[0, pl.ds(r, 8), :], taps_ref, cols)[:, :cols]
-        return c
-
-    lax.fori_loop(0, rows // 8, strip, 0)
+    toeplitz(taps_ref, 0, th_s, tl_s)
+    filter_pieces((up_ref, main_ref, down_ref), e_s, cols, 0, th_s, tl_s)
     left_ref[...] = jnp.zeros_like(left_ref)
     patches = prow_ref.shape[2]
     xcol = lax.broadcasted_iota(jnp.int32, (patches, cols), 1)
@@ -130,31 +191,18 @@
     lax.fori_loop(0, rows // CHUNK, chunk, 0)
 
 
-def k2(taps_ref, info_ref, up_ref, main_ref, down_ref, rcat_ref, w_ref, left_ref, e_s, *, first):
-    rows, cols = main_ref.shape[1:]
+def k2(taps_ref, info_ref, *refs, first, pieces, start):
+    piece_refs = refs[:pieces]
+    rcat_ref, w_ref, left_ref, e_s, th_s, tl_s = refs[pieces:]
+    rows = sum(p.shape[1] for p in piece_refs) - 2 * MARGIN
+    cols = w_ref.shape[2]
     t = pl.program_id(0) + first
-    band_start = info_ref[0]
+    band_start = info_ref[0] + start
     total_rows = info_ref[1]
     dy = info_ref[3 + 3 * t]
     dx = info_ref[4 + 3 * t]
-    wd = cols + PAD
-    turn = lax.rem(wd - dx, wd)
-    x = lax.broadcasted_iota(jnp.int32, (8, cols), 1) + dx
-    inside = (x >= 0) & (x < cols)
-
-    def place(v):
-        e = pltpu.roll(filter_strip(v, taps_ref, cols), turn, 1)[:, :cols]
-        return jnp.where(inside, e, 0.0)
-
-    e_s[0:8, :] = place(up_ref[0])
-    e_s[rows + 8 : rows + 16, :] = place(down_ref[0])
-
-    def strip(i, c):
-        r = pl.multiple_of(i * 8, 8)
-        e_s[pl.ds(r + 8, 8), :] = place(main_ref[0, pl.ds(r, 8), :])
-        return c
-
-    lax.fori_loop(0, rows // 8, strip, 0)
+    toeplitz(taps_ref, dx, th_s, tl_s)
+    filter_pieces(piece_refs, e_s, cols, dx, th_s, tl_s)
     left_ref[...] = jnp.zeros_like(left_ref)
     tm = band(taps_ref, dy)
     yl = lax.broadcasted_iota(jnp.int32, tm.shape, 0) + band_start + dy
@@ -163,12 +211,12 @@
         base = pl.multiple_of(c * CHUNK, CHUNK)
         y = yl + base
         tm_hi, tm_lo = split3(jnp.where((y >= 0) & (y < total_rows), tm, 0.0))
-        rc = rcat_ref[c]
+        rc = rcat_ref[c + start // CHUNK]
         for b in range(cols // COLB):
             cs = slice(b * COLB, (b + 1) * COLB)
             eh, el = split3(e_s[pl.ds(base, CHUNK + 2 * MARGIN), cs])
             q = mm(tm_hi, eh) + (mm(tm_hi, el) + mm(tm_lo, eh))
-            p = w_ref[0, pl.ds(base, CHUNK), cs] * q
+            p = w_ref[0, pl.ds(pl.multiple_of(base + start, CHUNK), CHUNK), cs] * q
             left_ref[0, :, cs] += mm(rc, split_rows(p))
         return carry
 
@@ -301,9 +349,14 @@
     tiles, tilts = lax.axis_size("tile"), lax.axis_size("tilt")
     nodes = cols_interp.shape[0]
     patches = patch_rows.shape[1]
-    raw_next = shifted(images[0], "tilt", -1)
-    low = shifted(images[:, rows - MARGIN :, :], "tile", 1)
-    high = shifted(images[:, :MARGIN, :], "tile", -1)
+    first_rows = rows - CHUNK + MARGIN
+    piece_a = images[0, :first_rows]
+    piece_b = images[0, first_rows:]
+    piece_a, piece_b, held = lax.optimization_barrier((piece_a, piece_b, images))
+    next_a = shifted(piece_a, "tilt", -1)
+    next_b = shifted(piece_b, "tilt", -1)
+    low = shifted(held[:, rows - MARGIN :, :], "tile", 1)
+    high = shifted(held[:, :MARGIN, :], "tile", -1)
     rim = shifted(jnp.concatenate([low[0], high[0]], axis=0), "tilt", -1)
 
     t_global = lax.axis_index("tilt") * tilt_count + jnp.arange(tilt_count, dtype=jnp.int32)
@@ -333,6 +386,7 @@
     def whole(shape):
         return pl.BlockSpec(shape, lambda i: (0,) * len(shape))
 
+    bands = [pltpu.VMEM((2 * WIDE, WIDE), BF16)] * 2
     e_scratch = pltpu.VMEM((rows + 2 * MARGIN, cols), F32)
     big = rows * cols
     w, w2, left_f = pl.pallas_call(
@@ -345,27 +399,29 @@
                    jax.ShapeDtypeStruct((tilt_count, rows, cols), F32),
                    jax.ShapeDtypeStruct((tilt_count, nodes, cols), F32)],
         scratch_shapes=[e_scratch, pltpu.VMEM((CHUNK, cols), F32), pltpu.VMEM((CHUNK, cols), F32),
-                        pltpu.VMEM((CHUNK, cols), F32), pltpu.VMEM((patches, cols), BF16)],
+                        pltpu.VMEM((CHUNK, cols), F32), pltpu.VMEM((patches, cols), BF16)] + bands,
         compiler_params=pltpu.CompilerParams(vmem_limit_bytes=vm),
         cost_estimate=pl.CostEstimate(flops=60 * big * tilt_count, bytes_accessed=40 * big * tilt_count,
                                       transcendentals=0),
         name="weigh",
     )(taps, info, patch_rows[:, None, :], patch_cols[:, :, None], low, images, high, rcat)
 
-    def partner(up, main, down, first, count, off):
+    def partner(pieces, first, count, off, start):
+        taken = sum(p.shape[1] for p in pieces)
+        area = (taken - 2 * MARGIN) * cols
         return pl.pallas_call(
-            functools.partial(k2, first=first),
+            functools.partial(k2, first=first, pieces=len(pieces), start=start),
             grid=(count,),
-            in_specs=[smem, smem, per((MARGIN, cols), off), per((rows, cols), off),
-                      per((MARGIN, cols), off), whole(rcat.shape), per((rows, cols), first)],
+            in_specs=[smem, smem] + [per(p.shape[1:], off) for p in pieces]
+            + [whole(rcat.shape), per((rows, cols), first)],
             out_specs=per((nodes, cols)),
             out_shape=jax.ShapeDtypeStruct((count, nodes, cols), F32),
-            scratch_shapes=[e_scratch],
+            scratch_shapes=[pltpu.VMEM((taken, cols), F32)] + bands,
             compiler_params=pltpu.CompilerParams(vmem_limit_bytes=vm),
-            cost_estimate=pl.CostEstimate(flops=40 * big * count, bytes_accessed=30 * big * count,
+            cost_estimate=pl.CostEstimate(flops=40 * area * count, bytes_accessed=30 * area * count,
                                           transcendentals=0),
             name="partner",
-        )(taps, info, up, main, down, rcat, w)
+        )(taps, info, *pieces, rcat, w)
 
     rt = rows_interp.T
 
@@ -404,12 +460,15 @@
     local = tilt_count - 1
     extra = ()
     if local:
-        lq = partner(low, images, high, 0, local, 1)
+        lq = partner((low, images, high), 0, local, 1, 0)
         extra = (step(lq, left_f, w2, False, 1),)
     else:
         extra = (jnp.zeros((1, nodes, nodes), F32),)
-    lq_last = partner(rim[None, :MARGIN], raw_next[None], rim[None, MARGIN:], tilt_count - 1, 1, 0)
-    return step(lq_last, left_f, w2, True, 2, extra)
+    last = tilt_count - 1
+    tail = first_rows - 2 * MARGIN
+    lq_a = partner((rim[None, :MARGIN], next_a[None]), last, 1, 0, 0)
+    lq_b = partner((next_a[None, tail:], next_b[None], rim[None, MARGIN:]), last, 1, 0, first_rows - MARGIN)
+    return step(lq_a + lq_b, left_f, w2, True, 2, extra)
 
 
 def solution(mesh):

time: 194 us -> 178 us (0.918)
  Pallas kernels: 173 us -> 141 us
  waiting for transfers between devices: 0.01 us -> 7.75 us
  local copies, waits for them, and re-layouts: 9.44 us -> 13.6 us
  other arithmetic: 3.65 us -> 6.01 us
    pallas_call x2 -> x3, Pallas kernels: 57 us -> 39.4 us  [partner(): pl.pallas_call(functools.partial(k2, first=first, pieces=len(pieces), sta...]
    pallas_call x1, Pallas kernels: 48.2 us -> 36.2 us  [shards(): pl.pallas_call(k1, grid=(tilt_count,), in_specs=[smem, smem, per((1, patc...]
    ppermute x4 -> x5, waiting for transfers between devices: 0.01 us -> 7.75 us  [shifted(): lax.ppermute(value, axis, [(source, source + steps) for source in range(i...]
    add x0 -> x1, other arithmetic: none -> 2.34 us  [shards(): return step(lq_a + lq_b, left_f, w2, True, 2, extra)]
    ppermute x4 -> x5, starting transfers between devices: 7.17 us -> 8.2 us  [shifted(): lax.ppermute(value, axis, [(source, source + steps) for source in range(i...]
    squeeze x1 -> x2, local copies, waits for them, and re-layouts: 4.61 us -> 5.31 us  [the longest x1 4.07 us: shards(): piece_a = images[0, :first_rows]]
  transfers between devices with their start and end apart: 4 -> 5, of which waited for: 0 -> 1; matrix products, arithmetic and copies ran while one was open for 6% -> 4% of each run, Pallas kernels for 55% -> 56%
where the time goes in v2:
time: 178 us; the launch traced here: 177 us
  Pallas kernels  141 us (79%)
  local copies, waits for them, and re-layouts  13.6 us (8%)
  starting transfers between devices  8.2 us (5%)
  waiting for transfers between devices  7.75 us (4%)
  other arithmetic  6.01 us (3%)
    pallas_call x2, Pallas kernels, step(): pl.pallas_call(functools.partial(refine, n=n, final=final, sizes=(tiles,...  65.8 us
    pallas_call x3, Pallas kernels, partner(): pl.pallas_call(functools.partial(k2, first=first, pieces=len(pieces), sta...  39.4 us
    pallas_call x1, Pallas kernels, shards(): pl.pallas_call(k1, grid=(tilt_count,), in_specs=[smem, smem, per((1, patc...  36.2 us
    ppermute x5, starting transfers between devices, shifted(): lax.ppermute(value, axis, [(source, source + steps) for source in range(i...  8.2 us
    ppermute x5, waiting for transfers between devices, shifted(): lax.ppermute(value, axis, [(source, source + steps) for source in range(i...  7.75 us
    squeeze x1, local copies, waits for them, and re-layouts, shards(): piece_a = images[0, :first_rows]  4.07 us
  transfers between devices with their start and end apart: 5, of which 1 were waited for; matrix products, arithmetic and copies ran while one was open for 4% of the time, Pallas kernels for 56%

profile of v2, /device:TPU:0, one launch (start us, length us, event | category | flops | bytes accessed | tf_op | source)
XLA Modules:
  0.0 177.2 jit_solution(3250734716216913590)
XLA Ops:
  0.0 0.0 copy-start
  0.0 4.1 %slice_bitcast_fusion = f32[200,4096]{1,0:T(8,128)} fusion(f32[2,256,4096]{2,1,0:T(8,128)} %refs_1_.1), kind=kLoop, calls=%fused_computation | loop fusion | bytes 6553600 | tf_op jit(solution)/shard_map/squeeze | solution.py:353
  4.1 1.2 slice_bitcast_fusion.1
  5.3 0.0 copy-start.6
  5.3 0.0 copy-start.5
  5.3 1.9 %fusion.2 = (f32[2,8,4096]{2,1,0:T(8,128)}, f32[2,8,4096]{2,1,0:T(8,128)}) fusion(f32[2,256,4096]{2,1,0:T(8,128)} %refs_1_.1), kind=kLoop, calls=%fused_computation.21 | loop fusion | bytes 1048576 | tf_op jit(solution)/shard_map/slice | solution.py:358
  7.3 1.3 collective-permute-start.1
  8.6 3.0 %collective-permute-start = (f32[2,8,4096]{2,1,0:T(8,128)}, f32[2,8,4096]{2,1,0:T(8,128)S(1)}, u32[]{:S(2)}, u32[]{:S(2)}) collective-permute-start(f32[2,8,4096]{2,1,0:T(8,128)} %get-tuple-element.17), channel_id=1, source_target_pairs={{0,1},{1,2},{2,3},{4,5},{5,6},{6,7},{8,9},{9,10},{10,11},{12,13},{... | collective-permute-start | bytes 786440 | tf_op jit(solution)/shard_map/ppermute | solution.py:28
  11.6 1.3 collective-permute-start.3
  12.9 1.3 collective-permute-start.4
  14.3 0.0 copy-done
  14.3 0.0 copy-start.7
  14.3 0.2 fusion
  14.4 1.3 pad_maximum_fusion.refs_4_
  15.8 0.0 copy-done.6
  15.8 0.1 pad_add_fusion
  15.9 0.1 reshape.19
  16.0 0.0 copy-done.5
  16.0 0.1 reshape.20
  16.1 0.0 collective-permute-done.1.down_ref.refs_2_
  16.1 0.0 copy-start.2
  16.2 0.0 collective-permute-done.up_ref.refs_0_
  16.2 0.0 copy-start.3
  16.2 1.3 collective-permute-start.2
  17.5 0.6 pad_add_fusion.1.info_ref
  18.1 0.7 copy.14
  18.8 0.0 copy-done.7
  18.8 0.7 copy.13.pcol_ref
  19.5 0.7 add_convert_fusion.refs_7_
  20.2 0.8 pad_maximum_fusion.2.rcat_ref.refs_2_.refs_3_.refs_6_
  21.0 0.0 copy-done.2
  21.0 0.0 copy-done.3
  21.0 36.2 %weigh.1 = (f32[2,256,4096]{2,1,0:T(8,128)}, f32[2,256,4096]{2,1,0:T(8,128)}, f32[2,64,4096]{2,1,0:T(8,128)}) custom-call(f32[9]{0:T(128)} %taps_ref.7, s32[8]{0:T(128)} %pad_add_fusion.1.info_ref, s32[2,1,16]{2,1,0:T(1,128)} %bitcast.28, s32[2,16,1]{2,1,0:T(8,128)} %copy.13.pcol_ref, f32[2,8,4096]{2,1,0:T(8,128)} %copy-done.3, f32[2,256,4096]{2,1,0:T(8,128)} %refs_1_.1, ...), custom_call_target="tpu_custom_call" | custom-call | flops 125829120 | bytes 83886080 | tf_op jit(solution)/shard_map/weigh/pallas_call | solution.py:392
  57.2 17.8 %partner.5.refs_0_ = f32[1,64,4096]{2,1,0:T(8,128)} custom-call(f32[9]{0:T(128)} %taps_ref.7, s32[8]{0:T(128)} %pad_add_fusion.1.info_ref, f32[2,8,4096]{2,1,0:T(8,128)} %copy-done.3, f32[2,256,4096]{2,1,0:T(8,128)} %refs_1_.1, f32[2,8,4096]{2,1,0:T(8,128)} %copy-done.2, bf16[4,64,192]{2,1,0:T(8,128)(2,1)} %pad_maximum_fusion.2.rcat_ref.refs_2_.refs_3_.refs_6_, ...), custom_call_target="tpu_custom_call" | custom-call | flops 41943040 | bytes 31457280 | tf_op jit(solution)/shard_map/partner/pallas_call | solution.py:412
  74.9 30.5 %refine_local.1.refs_8_ = f32[1,64,64]{2,1,0:T(8,128)} custom-call(f32[1,64,4096]{2,1,0:T(8,128)} %partner.5.refs_0_, f32[2,64,4096]{2,1,0:T(8,128)} %get-tuple-element.15.refs_1_, f32[2,256,4096]{2,1,0:T(8,128)} %get-tuple-element.16.refs_2_, f32[64,4096]{1,0:T(8,128)} %refs_3_.3, bf16[192,4096]{1,0:T(8,128)(2,1)} %pad_maximum_fusion.refs_4_, ...), custom_call_target="tpu_custom_call" | custom-call | flops 62914560 | bytes 41943040 | tf_op jit(solution)/shard_map/refine_local/pallas_call | solution.py:447
  105.4 7.7 %collective-permute-done.2 = f32[16,4096]{1,0:T(8,128)S(1)} collective-permute-done((f32[16,4096]{1,0:T(8,128)S(1)}, f32[16,4096]{1,0:T(8,128)S(1)}, u32[]{:S(2)}, u32[]{:S(2)}) %collective-permute-start.2) | collective-permute-done | bytes 262176 | tf_op jit(solution)/shard_map/ppermute | solution.py:28
  113.2 0.7 slice_bitcast_fusion.3
  113.9 0.0 collective-permute-done.3
  113.9 14.5 %partner.3 = f32[1,64,4096]{2,1,0:T(8,128)} custom-call(f32[9]{0:T(128)} %taps_ref.7, s32[8]{0:T(128)} %pad_add_fusion.1.info_ref, f32[1,8,4096]{2,1,0:T(8,128)} %get-tuple-element.22.refs_0_, f32[1,200,4096]{2,1,0:T(8,128)} %bitcast.6.refs_1_, bf16[4,64,192]{2,1,0:T(8,128)(2,1)} %pad_maximum_fusion.2.rcat_ref.refs_2_.refs_3_.refs_6_, ...), custom_call_target="tpu_custom_call" | custom-call | flops 31457280 | bytes 23592960 | tf_op jit(solution)/shard_map/partner/pallas_call | solution.py:412
  128.4 1.7 slice_bitcast_fusion.2.refs_0_
  130.1 0.0 collective-permute-done.4
  130.1 0.0 copy-start.4
  130.1 0.9 copy-done.4
  131.1 7.2 %partner.4 = f32[1,64,4096]{2,1,0:T(8,128)} custom-call(f32[9]{0:T(128)} %taps_ref.7, s32[8]{0:T(128)} %pad_add_fusion.1.info_ref, f32[1,16,4096]{2,1,0:T(8,128)} %slice_bitcast_fusion.2.refs_0_, f32[1,56,4096]{2,1,0:T(8,128)} %bitcast.27, f32[1,8,4096]{2,1,0:T(8,128)} %get-tuple-element.21.refs_2_, ...), custom_call_target="tpu_custom_call" | custom-call | flops 10485760 | bytes 7864320 | tf_op jit(solution)/shard_map/partner/pallas_call | solution.py:412
  138.2 0.0 copy-done.1
  138.2 2.3 %add.18.refs_0_ = f32[1,64,4096]{2,1,0:T(8,128)} add(f32[1,64,4096]{2,1,0:T(8,128)S(1)} %copy-done.1, f32[1,64,4096]{2,1,0:T(8,128)} %partner.4) | non-fusion elementwise | flops 262144 | bytes 3145728 | tf_op jit(solution)/shard_map/add | solution.py:471
  140.6 35.3 %refine_last.1 = f32[2,16,64]{2,1,0:T(8,128)} custom-call(f32[1,64,4096]{2,1,0:T(8,128)} %add.18.refs_0_, f32[2,64,4096]{2,1,0:T(8,128)} %get-tuple-element.15.refs_1_, f32[2,256,4096]{2,1,0:T(8,128)} %get-tuple-element.16.refs_2_, f32[64,4096]{1,0:T(8,128)} %refs_3_.3, bf16[192,4096]{1,0:T(8,128)(2,1)} %pad_maximum_fusion.refs_4_, f32[256,64]{1,0:T(8,128)} %bitcast.26, ...), custom_call_target="tpu_custom_call" | custom-call | flops 62914560 | bytes 41943040 | tf_op jit(solution)/shard_map/refine_last/pallas_call | solution.py:447
  175.9 1.3 copy.18
  (7 shorter events, 0.1 us)
Async XLA Ops:
  0.0 14.3 %copy-start = (f32[64,4096]{1,0:T(8,128)S(1)}, f32[64,4096]{1,0:T(8,128)}, u32[]{:S(2)}) copy-start(f32[64,4096]{1,0:T(8,128)} %refs_3_.3) | copy-start | bytes 3145732
  5.3 10.5 %copy-start.6 = (s32[2,2]{1,0:T(2,128)S(1)}, s32[2,2]{1,0:T(2,128)}, u32[]{:S(2)}) copy-start(s32[2,2]{1,0:T(2,128)} %param.9) | copy-start | bytes 52
  5.3 10.6 %copy-start.5 = (f32[64,256]{1,0:T(8,128)S(1)}, f32[64,256]{1,0:T(8,128)}, u32[]{:S(2)}) copy-start(f32[64,256]{1,0:T(8,128)} %param.12) | copy-start | bytes 196612
  7.3 8.8 %collective-permute-start.1 = (f32[2,8,4096]{2,1,0:T(8,128)}, f32[2,8,4096]{2,1,0:T(8,128)S(1)}, u32[]{:S(2)}, u32[]{:S(2)}) collective-permute-start(f32[2,8,4096]{2,1,0:T(8,128)} %get-tuple-element.18), channel_id=1, source_target_pairs={{1,0},{2,1},{3,2},{5,4},{6,5},{7,6},{9,8},{10,9},{11,10},{13,12},{... | collective-permute-start | bytes 786440 | tf_op jit(solution)/shard_map/ppermute | solution.py:28
  8.6 7.6 %collective-permute-start = (f32[2,8,4096]{2,1,0:T(8,128)}, f32[2,8,4096]{2,1,0:T(8,128)S(1)}, u32[]{:S(2)}, u32[]{:S(2)}) collective-permute-start(f32[2,8,4096]{2,1,0:T(8,128)} %get-tuple-element.17), channel_id=1, source_target_pairs={{0,1},{1,2},{2,3},{4,5},{5,6},{6,7},{8,9},{9,10},{10,11},{12,13},{... | collective-permute-start | bytes 786440 | tf_op jit(solution)/shard_map/ppermute | solution.py:28
  11.6 102.3 %collective-permute-start.3 = (f32[200,4096]{1,0:T(8,128)}, f32[200,4096]{1,0:T(8,128)}, u32[]{:S(2)}, u32[]{:S(2)}) collective-permute-start(f32[200,4096]{1,0:T(8,128)} %slice_bitcast_fusion), channel_id=1, source_target_pairs={{4,0},{8,4},{12,8},{16,12},{20,16},{24,20},{28,24},{5,1},{9,5},{13... | collective-permute-start | bytes 9830408 | tf_op jit(solution)/shard_map/ppermute | solution.py:28
  12.9 117.2 %collective-permute-start.4 = (f32[56,4096]{1,0:T(8,128)S(1)}, f32[56,4096]{1,0:T(8,128)S(1)}, u32[]{:S(2)}, u32[]{:S(2)}) collective-permute-start(f32[56,4096]{1,0:T(8,128)S(1)} %slice_bitcast_fusion.1), channel_id=1, source_target_pairs={{4,0},{8,4},{12,8},{16,12},{20,16},{24,20},{28,24},{5,1},{9,5},{13... | collective-permute-start | bytes 2752520 | tf_op jit(solution)/shard_map/ppermute | solution.py:28
  14.3 4.6 %copy-start.7 = (s32[2,16]{1,0:T(2,128)S(1)}, s32[2,16]{1,0:T(2,128)}, u32[]{:S(2)}) copy-start(s32[2,16]{1,0:T(2,128)} %param.11) | copy-start | bytes 388
  16.1 4.9 %copy-start.2 = (f32[2,8,4096]{2,1,0:T(8,128)}, f32[2,8,4096]{2,1,0:T(8,128)S(1)}, u32[]{:S(2)}) copy-start(f32[2,8,4096]{2,1,0:T(8,128)S(1)} %collective-permute-done.1.down_ref.refs_2_) | copy-start | bytes 786436
  16.2 4.8 %copy-start.3 = (f32[2,8,4096]{2,1,0:T(8,128)}, f32[2,8,4096]{2,1,0:T(8,128)S(1)}, u32[]{:S(2)}) copy-start(f32[2,8,4096]{2,1,0:T(8,128)S(1)} %collective-permute-done.up_ref.refs_0_) | copy-start | bytes 786436
  16.2 96.9 %collective-permute-start.2 = (f32[16,4096]{1,0:T(8,128)S(1)}, f32[16,4096]{1,0:T(8,128)S(1)}, u32[]{:S(2)}, u32[]{:S(2)}) collective-permute-start(f32[16,4096]{1,0:T(8,128)S(1)} %pad_maximum_fusion.1), channel_id=1, source_target_pairs={{4,0},{8,4},{12,8},{16,12},{20,16},{24,20},{28,24},{5,1},{9,5},{13... | collective-permute-start | bytes 786440 | tf_op jit(solution)/shard_map/ppermute | solution.py:28
  130.1 0.9 copy-start.4
  131.1 7.2 %copy-start.1 = (f32[1,64,4096]{2,1,0:T(8,128)S(1)}, f32[1,64,4096]{2,1,0:T(8,128)}, u32[]{:S(2)}) copy-start(f32[1,64,4096]{2,1,0:T(8,128)} %partner.3) | copy-start | bytes 3145732

commit v3 on v2

--- a/solution.py
+++ b/solution.py
@@ -6,6 +6,7 @@
 from jax.experimental import pallas as pl
 from jax.experimental.pallas import tpu as pltpu
 from jax.sharding import PartitionSpec as P
+
 
 RAD = 4
 SMAX = 4
@@ -44,12 +45,6 @@
     )
 
 
-def mm_hi_t(a, b):
-    return lax.dot_general(
-        a, b, (((1,), (1,)), ((), ())), precision=HI, preferred_element_type=F32
-    )
-
-
 def toeplitz(taps_ref, dx, th_s, tl_s):
     i = lax.broadcasted_iota(jnp.int32, (2 * WIDE, WIDE), 0)
     o = lax.broadcasted_iota(jnp.int32, (2 * WIDE, WIDE), 1)
@@ -128,13 +123,20 @@
 
 def band(taps_ref, dy):
     ext = CHUNK + 2 * MARGIN
-    y = lax.broadcasted_iota(jnp.int32, (CHUNK, ext), 0)
-    j = lax.broadcasted_iota(jnp.int32, (CHUNK, ext), 1)
+    y = lax.broadcasted_iota(jnp.int32, (CHUNK, 3 * ext), 0)
+    j = lax.broadcasted_iota(jnp.int32, (CHUNK, 3 * ext), 1)
+    j = jnp.where(j >= 2 * ext, j - 2 * ext, jnp.where(j >= ext, j - ext, j))
     d = j - y - (MARGIN - RAD) - dy
-    out = jnp.zeros((CHUNK, ext), F32)
+    out = jnp.zeros((CHUNK, 3 * ext), F32)
     for k in range(2 * RAD + 1):
         out = jnp.where(d == k, taps_ref[k], out)
     return out
+
+
+def stacked(m):
+    hi, lo = split3(m)
+    lane = lax.broadcasted_iota(jnp.int32, m.shape, 1)
+    return jnp.where(lane < 2 * m.shape[1] // 3, hi.astype(F32), lo.astype(F32)).astype(BF16)
 
 
 def split3(m):
@@ -155,7 +157,7 @@
     patches = prow_ref.shape[2]
     xcol = lax.broadcasted_iota(jnp.int32, (patches, cols), 1)
     cb_s[...] = (jnp.abs(xcol - pcol_ref[0]) <= PATCH_HALF).astype(F32).astype(BF16)
-    tm_hi, tm_lo = split3(band(taps_ref, 0))
+    tm = stacked(band(taps_ref, 0))
 
     def chunk(c, carry):
         base = pl.multiple_of(c * CHUNK, CHUNK)
@@ -164,8 +166,7 @@
         for b in range(cols // COLB):
             cs = slice(b * COLB, (b + 1) * COLB)
             e = e_s[pl.ds(base, CHUNK + 2 * MARGIN), cs]
-            eh, el = split3(e)
-            f_s[:, cs] = mm(tm_hi, eh) + (mm(tm_hi, el) + mm(tm_lo, eh))
+            f_s[:, cs] = mm(tm, split_rows(e))
             m_s[:, cs] = mm(rb, cb_s[:, cs])
 
         def weigh(i, cc):
@@ -178,7 +179,7 @@
             ro = pl.multiple_of(base + r, 8)
             w_ref[0, pl.ds(ro, 8), :] = w
             w2_ref[0, pl.ds(ro, 8), :] = w * gx
-            p_s[pl.ds(r, 8), :] = w * f
+            p_s[pl.ds(r, 8), :] = -(w * f)
             return cc
 
         lax.fori_loop(0, CHUNK // 8, weigh, 0)
@@ -193,7 +194,7 @@
 
 def k2(taps_ref, info_ref, *refs, first, pieces, start):
     piece_refs = refs[:pieces]
-    rcat_ref, w_ref, left_ref, e_s, th_s, tl_s = refs[pieces:]
+    rcat_ref, w_ref, init_ref, left_ref, e_s, th_s, tl_s = refs[pieces:]
     rows = sum(p.shape[1] for p in piece_refs) - 2 * MARGIN
     cols = w_ref.shape[2]
     t = pl.program_id(0) + first
@@ -203,19 +204,18 @@
     dx = info_ref[4 + 3 * t]
     toeplitz(taps_ref, dx, th_s, tl_s)
     filter_pieces(piece_refs, e_s, cols, dx, th_s, tl_s)
-    left_ref[...] = jnp.zeros_like(left_ref)
+    left_ref[...] = init_ref[...]
     tm = band(taps_ref, dy)
     yl = lax.broadcasted_iota(jnp.int32, tm.shape, 0) + band_start + dy
 
     def chunk(c, carry):
         base = pl.multiple_of(c * CHUNK, CHUNK)
         y = yl + base
-        tm_hi, tm_lo = split3(jnp.where((y >= 0) & (y < total_rows), tm, 0.0))
+        tc = stacked(jnp.where((y >= 0) & (y < total_rows), tm, 0.0))
         rc = rcat_ref[c + start // CHUNK]
         for b in range(cols // COLB):
             cs = slice(b * COLB, (b + 1) * COLB)
-            eh, el = split3(e_s[pl.ds(base, CHUNK + 2 * MARGIN), cs])
-            q = mm(tm_hi, eh) + (mm(tm_hi, el) + mm(tm_lo, eh))
+            q = mm(tc, split_rows(e_s[pl.ds(base, CHUNK + 2 * MARGIN), cs]))
             p = w_ref[0, pl.ds(pl.multiple_of(base + start, CHUNK), CHUNK), cs] * q
             left_ref[0, :, cs] += mm(rc, split_rows(p))
         return carry
@@ -225,13 +225,13 @@
 
 def refine(*refs, n, final, sizes):
     if final:
-        (lq_ref, lf_ref, w2_ref, c_ref, ccat_ref, rt_ref, rcat_ref, sel_ref, gl_ref, out_ref,
+        (lq_ref, w2_ref, ccat_ref, rt_ref, r2_ref, sel_ref, gl_ref, out_ref,
          left_s, cat_s, acc_s, send_s, slots, csend_s, cslots, ssem, rsem, csem, crsem) = refs
     else:
-        (lq_ref, lf_ref, w2_ref, c_ref, ccat_ref, rt_ref, rcat_ref, sel_ref, out_ref,
+        (lq_ref, w2_ref, ccat_ref, rt_ref, r2_ref, sel_ref, out_ref,
          left_s, cat_s, acc_s, send_s, slots, ssem, rsem) = refs
     tiles, tilts = sizes
-    nodes, cols = c_ref.shape
+    nodes, cols = lq_ref.shape[1:]
     rows = rt_ref.shape[0]
     me = lax.axis_index("tile")
     place = lax.axis_index("tilt")
@@ -262,41 +262,41 @@
             total = total + slots[rnd, k]
         return total
 
+    def project(left):
+        hi, lo = split3(left)
+        q = lax.dot_general(jnp.concatenate([hi, lo], axis=0), ccat_ref[: 2 * nodes, :],
+                            (((1,), (1,)), ((), ())), preferred_element_type=F32)
+        q = q[:nodes] + q[nodes:]
+        return (q + pltpu.roll(q, nodes, 1))[:, :nodes]
+
     def direction(g, w2, apply):
-        g3 = mm_hi(mm_hi(rt_ref[...], g), sel_ref[...])
-        hi, lo = split3(g3)
-        lane = lax.broadcasted_iota(jnp.int32, g3.shape, 1)
-        cat_s[...] = jnp.where(lane < 2 * nodes, hi.astype(F32), lo.astype(F32)).astype(BF16)
+        cat_s[...] = stacked(mm_hi(rt_ref[...], mm_hi(g, sel_ref[...])))
         acc_s[...] = jnp.zeros_like(acc_s)
-        if apply:
-            left_s[...] = jnp.zeros_like(left_s)
-
-        def chunk(c, carry):
-            base = pl.multiple_of(c * CHUNK, CHUNK)
-            gc = cat_s[pl.ds(base, CHUNK), :]
-            rc = rcat_ref[c]
-            for b in range(cols // COLB):
-                cs = slice(b * COLB, (b + 1) * COLB)
-                v = mm(gc, ccat_ref[:, cs])
-                y = w2_ref[w2, pl.ds(base, CHUNK), cs] * v
-                acc_s[...] += y * v
-                if apply:
-                    left_s[:, cs] += mm(rc, split_rows(y))
+
+        def block(b, carry):
+            cs = pl.ds(pl.multiple_of(b * COLB, COLB), COLB)
+            v = mm(cat_s[...], ccat_ref[:, cs])
+            y = w2_ref[w2, :, cs] * v
+            acc_s[...] += jnp.sum((y * v).reshape(rows // 8, 8, COLB), axis=0)
+            if apply:
+                yh, yl = split3(y)
+                top = mm(r2_ref[...], yh)
+                left_s[:, cs] = top[:nodes] + (top[nodes:] + mm(r2_ref[:nodes, :], yl))
             return carry
 
-        lax.fori_loop(0, rows // CHUNK, chunk, 0)
+        lax.fori_loop(0, cols // COLB, block, 0)
         return jnp.sum(acc_s[...])
 
     grids = []
     for s in range(n):
         r = 3 * s
         send_s[r] = jnp.zeros_like(send_s[r])
-        send_s[r, :nodes, :nodes] = mm_hi_t(lq_ref[s] - lf_ref[s], c_ref[...])
+        send_s[r, :nodes, :nodes] = project(lq_ref[s])
         g1 = exchange(r)[:nodes, :nodes]
         gg1 = jnp.sum(g1 * g1)
         jj1 = direction(g1, s, True)
         send_s[r + 1] = jnp.zeros_like(send_s[r + 1])
-        send_s[r + 1, :nodes, :nodes] = mm_hi_t(left_s[...], c_ref[...])
+        send_s[r + 1, :nodes, :nodes] = project(left_s[...])
         send_s[r + 1, nodes : nodes + 8, :] = jnp.full((8, send_s.shape[2]), jj1, F32)
         both = exchange(r + 1)
         h1 = both[:nodes, :nodes]
@@ -354,10 +354,10 @@
     piece_b = images[0, first_rows:]
     piece_a, piece_b, held = lax.optimization_barrier((piece_a, piece_b, images))
     next_a = shifted(piece_a, "tilt", -1)
-    next_b = shifted(piece_b, "tilt", -1)
     low = shifted(held[:, rows - MARGIN :, :], "tile", 1)
     high = shifted(held[:, :MARGIN, :], "tile", -1)
     rim = shifted(jnp.concatenate([low[0], high[0]], axis=0), "tilt", -1)
+    next_b = shifted(piece_b, "tilt", -1)
 
     t_global = lax.axis_index("tilt") * tilt_count + jnp.arange(tilt_count, dtype=jnp.int32)
     valid = (t_global < tilt_count * tilts - 1).astype(jnp.int32)
@@ -406,14 +406,14 @@
         name="weigh",
     )(taps, info, patch_rows[:, None, :], patch_cols[:, :, None], low, images, high, rcat)
 
-    def partner(pieces, first, count, off, start):
+    def partner(pieces, init, at, first, count, off, start):
         taken = sum(p.shape[1] for p in pieces)
         area = (taken - 2 * MARGIN) * cols
         return pl.pallas_call(
             functools.partial(k2, first=first, pieces=len(pieces), start=start),
             grid=(count,),
             in_specs=[smem, smem] + [per(p.shape[1:], off) for p in pieces]
-            + [whole(rcat.shape), per((rows, cols), first)],
+            + [whole(rcat.shape), per((rows, cols), first), per((nodes, cols), at)],
             out_specs=per((nodes, cols)),
             out_shape=jax.ShapeDtypeStruct((count, nodes, cols), F32),
             scratch_shapes=[pltpu.VMEM((taken, cols), F32)] + bands,
@@ -421,14 +421,16 @@
             cost_estimate=pl.CostEstimate(flops=40 * area * count, bytes_accessed=30 * area * count,
                                           transcendentals=0),
             name="partner",
-        )(taps, info, *pieces, rcat, w)
+        )(taps, info, *pieces, rcat, w, init)
 
     rt = rows_interp.T
-
-    def step(lq, lf, w2s, final, cid, extra=()):
+    gh, gl = halves(rows_interp)
+    r2 = jnp.concatenate([gh, gl], axis=0)
+
+    def step(lq, w2s, final, cid, extra=()):
         n = lq.shape[0]
         scratch = [pltpu.VMEM((nodes, cols), F32), pltpu.VMEM((rows, 3 * nodes), BF16),
-                   pltpu.VMEM((CHUNK, COLB), F32), pltpu.VMEM((3 * n, nodes + 8, 128), F32),
+                   pltpu.VMEM((8, COLB), F32), pltpu.VMEM((3 * n, nodes + 8, 128), F32),
                    pltpu.VMEM((3 * n, tiles, nodes + 8, 128), F32)]
         sems = [pltpu.SemaphoreType.DMA((3 * n, tiles - 1)), pltpu.SemaphoreType.DMA((3 * n, tiles - 1))]
         if final:
@@ -440,10 +442,9 @@
         else:
             out = jax.ShapeDtypeStruct((n, nodes, nodes), F32)
         off = tilt_count - 1 if final else 0
-        args = (lq, lf, w2s, cols_interp, ccat, rt, rcat, sel) + tuple(extra)
-        specs = [whole(lq.shape), pl.BlockSpec((n,) + lf.shape[1:], lambda i: (off, 0, 0)),
-                 pl.BlockSpec((n,) + w2s.shape[1:], lambda i: (off, 0, 0))]
-        specs += [whole(a.shape) for a in args[3:]]
+        args = (lq, w2s, ccat, rt, r2, sel) + tuple(extra)
+        specs = [whole(lq.shape), pl.BlockSpec((n,) + w2s.shape[1:], lambda i: (off, 0, 0))]
+        specs += [whole(a.shape) for a in args[2:]]
         return pl.pallas_call(
             functools.partial(refine, n=n, final=final, sizes=(tiles, tilts)),
             grid=(1,),
@@ -460,15 +461,16 @@
     local = tilt_count - 1
     extra = ()
     if local:
-        lq = partner((low, images, high), 0, local, 1, 0)
-        extra = (step(lq, left_f, w2, False, 1),)
+        lq = partner((low, images, high), left_f, 0, 0, local, 1, 0)
+        extra = (step(lq, w2, False, 1),)
     else:
         extra = (jnp.zeros((1, nodes, nodes), F32),)
     last = tilt_count - 1
     tail = first_rows - 2 * MARGIN
-    lq_a = partner((rim[None, :MARGIN], next_a[None]), last, 1, 0, 0)
-    lq_b = partner((next_a[None, tail:], next_b[None], rim[None, MARGIN:]), last, 1, 0, first_rows - MARGIN)
-    return step(lq_a + lq_b, left_f, w2, True, 2, extra)
+    lq_a = partner((rim[None, :MARGIN], next_a[None]), left_f, last, last, 1, 0, 0)
+    lq_b = partner((next_a[None, tail:], next_b[None], rim[None, MARGIN:]), lq_a, 0, last, 1, 0,
+                   first_rows - MARGIN)
+    return step(lq_b, w2, True, 2, extra)
 
 
 def solution(mesh):

time: 178 us -> 174 us (0.978)
  Pallas kernels: 141 us -> 133 us
  waiting for transfers between devices: 7.75 us -> 0.01 us
  local copies, waits for them, and re-layouts: 13.6 us -> 19.3 us
  other arithmetic: 6.01 us -> 11 us
    ppermute x5, waiting for transfers between devices: 7.75 us -> 0.01 us  [shifted(): lax.ppermute(value, axis, [(source, source + steps) for source in range(i...]
    pallas_call x2, Pallas kernels: 65.8 us -> 59.2 us  [step(): pl.pallas_call(functools.partial(refine, n=n, final=final, sizes=(tiles,...]
    convert_element_type x2 -> x3, other arithmetic: 0.18 us -> 4.43 us  [halves(): return (hi.astype(BF16), (x - hi).astype(BF16))]
    add x1 -> x0, other arithmetic: 2.34 us -> none  [shards(): return step(lq_a + lq_b, left_f, w2, True, 2, extra)]
    unnamed x18 -> x10, local copies, waits for them, and re-layouts: 3.05 us -> 4.62 us
  transfers between devices with their start and end apart: 5 -> 5, of which waited for: 1 -> 0; matrix products, arithmetic and copies ran while one was open for 4% -> 12% of each run, Pallas kernels for 56% -> 53%
where the time goes in v3:
time: 174 us; the launch traced here: 173 us
  Pallas kernels  133 us (76%)
  local copies, waits for them, and re-layouts  19.3 us (11%)
  other arithmetic  11 us (6%)
  starting transfers between devices  9 us (5%)
    pallas_call x2, Pallas kernels, step(): pl.pallas_call(functools.partial(refine, n=n, final=final, sizes=(tiles,...  59.2 us
    pallas_call x3, Pallas kernels, partner(): pl.pallas_call(functools.partial(k2, first=first, pieces=len(pieces), sta...  38.2 us
    pallas_call x1, Pallas kernels, shards(): pl.pallas_call(k1, grid=(tilt_count,), in_specs=[smem, smem, per((1, patc...  36 us
    ppermute x5, starting transfers between devices, shifted(): lax.ppermute(value, axis, [(source, source + steps) for source in range(i...  9 us
    unnamed x10, local copies, waits for them, and re-layouts  4.62 us
    convert_element_type x3, other arithmetic, halves(): return (hi.astype(BF16), (x - hi).astype(BF16))  4.43 us
    squeeze x1, local copies, waits for them, and re-layouts, shards(): piece_a = images[0, :first_rows]  3.94 us
  transfers between devices with their start and end apart: 5, of which 0 were waited for; matrix products, arithmetic and copies ran while one was open for 12% of the time, Pallas kernels for 53%

profile of v3, /device:TPU:0, one launch (start us, length us, event | category | flops | bytes accessed | tf_op | source)
XLA Modules:
  0.0 172.8 jit_solution(6961218489691280237)
XLA Ops:
  0.0 3.9 %slice_bitcast_fusion = f32[200,4096]{1,0:T(8,128)} fusion(f32[2,256,4096]{2,1,0:T(8,128)} %refs_1_.1), kind=kLoop, calls=%fused_computation | loop fusion | bytes 6553600 | tf_op jit(solution)/shard_map/squeeze | solution.py:353
  3.9 2.2 %slice_bitcast_fusion.1 = f32[56,4096]{1,0:T(8,128)} fusion(f32[2,256,4096]{2,1,0:T(8,128)} %refs_1_.1), kind=kLoop, calls=%fused_computation.5 | loop fusion | bytes 1835008 | tf_op jit(solution)/shard_map/squeeze | solution.py:354
  6.1 0.0 copy-start.2
  6.1 1.4 collective-permute-start
  7.5 1.3 collective-permute-start.1
  8.8 1.9 %fusion.3 = (f32[2,8,4096]{2,1,0:T(8,128)}, f32[2,8,4096]{2,1,0:T(8,128)}) fusion(f32[2,256,4096]{2,1,0:T(8,128)} %refs_1_.1), kind=kLoop, calls=%fused_computation.25 | loop fusion | bytes 1048576 | tf_op jit(solution)/shard_map/slice | solution.py:357
  10.7 1.3 collective-permute-start.3
  12.0 3.7 %collective-permute-start.2 = (f32[2,8,4096]{2,1,0:T(8,128)}, f32[2,8,4096]{2,1,0:T(8,128)}, u32[]{:S(2)}, u32[]{:S(2)}) collective-permute-start(f32[2,8,4096]{2,1,0:T(8,128)} %get-tuple-element.17), channel_id=1, source_target_pairs={{0,1},{1,2},{2,3},{4,5},{5,6},{6,7},{8,9},{9,10},{10,11},{12,13},{... | collective-permute-start | bytes 786440 | tf_op jit(solution)/shard_map/ppermute | solution.py:29
  15.8 0.0 copy-start.3
  15.8 1.4 fusion
  17.2 1.5 reduce-precision_convert_fusion.2
  18.6 0.7 add_convert_fusion.refs_5_
  19.3 1.3 pad_maximum_fusion.refs_2_
  20.7 0.0 copy-done.2
  20.7 0.1 pad_add_fusion
  20.8 1.6 reshape.20
  22.4 0.1 reshape.19
  22.4 1.6 reduce-precision_convert_fusion.1
  24.0 0.0 collective-permute-done.3.down_ref.refs_2_
  24.0 0.0 copy-start.1
  24.0 0.0 collective-permute-done.2.up_ref.refs_0_
  24.1 1.0 slice_bitcast_fusion.6
  25.1 0.7 pad_maximum_fusion.1
  25.8 1.3 collective-permute-start.4
  27.1 0.6 pad_add_fusion.1.info_ref
  27.7 1.6 copy.14
  29.3 0.0 copy-done.3
  29.3 0.7 copy.13.pcol_ref
  30.0 1.4 pad_maximum_fusion.3.refs_4_
  31.4 1.7 pad_maximum_fusion.2.rcat_ref.refs_2_.refs_3_
  33.1 0.0 copy-done.1
  33.1 36.0 %weigh.1 = (f32[2,256,4096]{2,1,0:T(8,128)}, f32[2,256,4096]{2,1,0:T(8,128)}, f32[2,64,4096]{2,1,0:T(8,128)}) custom-call(f32[9]{0:T(128)} %taps_ref.7, s32[8]{0:T(128)} %pad_add_fusion.1.info_ref, s32[2,1,16]{2,1,0:T(1,128)} %bitcast.28, s32[2,16,1]{2,1,0:T(8,128)} %copy.13.pcol_ref, f32[2,8,4096]{2,1,0:T(8,128)} %collective-permute-done.2.up_ref.refs_0_, ...), custom_call_target="tpu_custom_call" | custom-call | flops 125829120 | bytes 83886080 | tf_op jit(solution)/shard_map/weigh/pallas_call | solution.py:392
  69.0 17.1 %partner.5.refs_0_ = f32[1,64,4096]{2,1,0:T(8,128)} custom-call(f32[9]{0:T(128)} %taps_ref.7, s32[8]{0:T(128)} %pad_add_fusion.1.info_ref, f32[2,8,4096]{2,1,0:T(8,128)} %collective-permute-done.2.up_ref.refs_0_, f32[2,256,4096]{2,1,0:T(8,128)} %refs_1_.1, f32[2,8,4096]{2,1,0:T(8,128)} %copy-done.1, ...), custom_call_target="tpu_custom_call" | custom-call | flops 41943040 | bytes 31457280 | tf_op jit(solution)/shard_map/partner/pallas_call | solution.py:412
  86.1 24.9 %refine_local.1.refs_6_ = f32[1,64,64]{2,1,0:T(8,128)} custom-call(f32[1,64,4096]{2,1,0:T(8,128)} %partner.5.refs_0_, f32[2,256,4096]{2,1,0:T(8,128)} %get-tuple-element.16.refs_1_, bf16[192,4096]{1,0:T(8,128)(2,1)} %pad_maximum_fusion.refs_2_, f32[256,64]{1,0:T(8,128)} %bitcast.26, bf16[128,256]{1,0:T(8,128)(2,1)} %pad_maximum_fusion.3.refs_4_, ...), custom_call_target="tpu_custom_call" | custom-call | flops 62914560 | bytes 41943040 | tf_op jit(solution)/shard_map/refine_local/pallas_call | solution.py:448
  111.1 0.0 collective-permute-done.4
  111.1 1.7 slice_bitcast_fusion.3
  112.7 0.0 collective-permute-done
  112.7 0.0 copy-start
  112.7 1.7 copy-done
  114.4 13.9 %partner.3.refs_5_ = f32[1,64,4096]{2,1,0:T(8,128)} custom-call(f32[9]{0:T(128)} %taps_ref.7, s32[8]{0:T(128)} %pad_add_fusion.1.info_ref, f32[1,8,4096]{2,1,0:T(8,128)} %get-tuple-element.21.refs_0_, f32[1,200,4096]{2,1,0:T(8,128)} %bitcast.25, bf16[4,64,192]{2,1,0:T(8,128)(2,1)} %pad_maximum_fusion.2.rcat_ref.refs_2_.refs_3_, ...), custom_call_target="tpu_custom_call" | custom-call | flops 31457280 | bytes 23592960 | tf_op jit(solution)/shard_map/partner/pallas_call | solution.py:412
  128.4 1.7 slice_bitcast_fusion.2.refs_0_
  130.0 0.0 collective-permute-done.1
  130.0 7.1 %partner.4.refs_0_ = f32[1,64,4096]{2,1,0:T(8,128)} custom-call(f32[9]{0:T(128)} %taps_ref.7, s32[8]{0:T(128)} %pad_add_fusion.1.info_ref, f32[1,16,4096]{2,1,0:T(8,128)} %slice_bitcast_fusion.2.refs_0_, f32[1,56,4096]{2,1,0:T(8,128)} %bitcast.4.refs_1_, f32[1,8,4096]{2,1,0:T(8,128)} %get-tuple-element.22.refs_2_, ...), custom_call_target="tpu_custom_call" | custom-call | flops 10485760 | bytes 7864320 | tf_op jit(solution)/shard_map/partner/pallas_call | solution.py:412
  137.2 34.3 %refine_last.1 = f32[2,16,64]{2,1,0:T(8,128)} custom-call(f32[1,64,4096]{2,1,0:T(8,128)} %partner.4.refs_0_, f32[2,256,4096]{2,1,0:T(8,128)} %get-tuple-element.16.refs_1_, bf16[192,4096]{1,0:T(8,128)(2,1)} %pad_maximum_fusion.refs_2_, f32[256,64]{1,0:T(8,128)} %bitcast.27, bf16[128,256]{1,0:T(8,128)(2,1)} %pad_maximum_fusion.3.refs_4_, ...), custom_call_target="tpu_custom_call" | custom-call | flops 62914560 | bytes 41943040 | tf_op jit(solution)/shard_map/refine_last/pallas_call | solution.py:448
  171.5 1.3 copy.18
  (3 shorter events, 0.0 us)
Async XLA Ops:
  6.1 14.6 %copy-start.2 = (s32[2,2]{1,0:T(2,128)S(1)}, s32[2,2]{1,0:T(2,128)}, u32[]{:S(2)}) copy-start(s32[2,2]{1,0:T(2,128)} %param.9) | copy-start | bytes 52
  6.1 106.6 %collective-permute-start = (f32[200,4096]{1,0:T(8,128)}, f32[200,4096]{1,0:T(8,128)S(1)}, u32[]{:S(2)}, u32[]{:S(2)}) collective-permute-start(f32[200,4096]{1,0:T(8,128)} %slice_bitcast_fusion), channel_id=1, source_target_pairs={{4,0},{8,4},{12,8},{16,12},{20,16},{24,20},{28,24},{5,1},{9,5},{13... | collective-permute-start | bytes 9830408 | tf_op jit(solution)/shard_map/ppermute | solution.py:29
  7.5 122.5 %collective-permute-start.1 = (f32[56,4096]{1,0:T(8,128)}, f32[56,4096]{1,0:T(8,128)}, u32[]{:S(2)}, u32[]{:S(2)}) collective-permute-start(f32[56,4096]{1,0:T(8,128)} %slice_bitcast_fusion.1), channel_id=1, source_target_pairs={{4,0},{8,4},{12,8},{16,12},{20,16},{24,20},{28,24},{5,1},{9,5},{13... | collective-permute-start | bytes 2752520 | tf_op jit(solution)/shard_map/ppermute | solution.py:29
  10.7 13.3 %collective-permute-start.3 = (f32[2,8,4096]{2,1,0:T(8,128)}, f32[2,8,4096]{2,1,0:T(8,128)S(1)}, u32[]{:S(2)}, u32[]{:S(2)}) collective-permute-start(f32[2,8,4096]{2,1,0:T(8,128)} %get-tuple-element.18), channel_id=1, source_target_pairs={{1,0},{2,1},{3,2},{5,4},{6,5},{7,6},{9,8},{10,9},{11,10},{13,12},{... | collective-permute-start | bytes 786440 | tf_op jit(solution)/shard_map/ppermute | solution.py:29
  12.0 12.0 %collective-permute-start.2 = (f32[2,8,4096]{2,1,0:T(8,128)}, f32[2,8,4096]{2,1,0:T(8,128)}, u32[]{:S(2)}, u32[]{:S(2)}) collective-permute-start(f32[2,8,4096]{2,1,0:T(8,128)} %get-tuple-element.17), channel_id=1, source_target_pairs={{0,1},{1,2},{2,3},{4,5},{5,6},{6,7},{8,9},{9,10},{10,11},{12,13},{... | collective-permute-start | bytes 786440 | tf_op jit(solution)/shard_map/ppermute | solution.py:29
  15.8 13.5 %copy-start.3 = (s32[2,16]{1,0:T(2,128)S(1)}, s32[2,16]{1,0:T(2,128)}, u32[]{:S(2)}) copy-start(s32[2,16]{1,0:T(2,128)} %param.11) | copy-start | bytes 388
  24.0 9.0 %copy-start.1 = (f32[2,8,4096]{2,1,0:T(8,128)}, f32[2,8,4096]{2,1,0:T(8,128)S(1)}, u32[]{:S(2)}) copy-start(f32[2,8,4096]{2,1,0:T(8,128)S(1)} %collective-permute-done.3.down_ref.refs_2_) | copy-start | bytes 786436
  25.8 85.3 %collective-permute-start.4 = (f32[16,4096]{1,0:T(8,128)}, f32[16,4096]{1,0:T(8,128)}, u32[]{:S(2)}, u32[]{:S(2)}) collective-permute-start(f32[16,4096]{1,0:T(8,128)} %pad_maximum_fusion.1), channel_id=1, source_target_pairs={{4,0},{8,4},{12,8},{16,12},{20,16},{24,20},{28,24},{5,1},{9,5},{13... | collective-permute-start | bytes 786440 | tf_op jit(solution)/shard_map/ppermute | solution.py:29
  112.7 1.7 copy-start
